TPU v7x, 128 devices: a whole 4x4x4 slice. The times are simulated.
128 devices in a mesh: surf: 16 (over y, z), depth: 8 (over x, core).
Axes of the slice: x: 4, y: 4, z: 4, core: 2. Of those that a mesh axis runs over, the one named last changes fastest.
Arguments:
- wave_now: float32 [4, 128, 128, 128], P(None, 'surf', 'depth'), may hold values from -6 to 6
- wave_old: float32 [4, 128, 128, 128], P(None, 'surf', 'depth'), may hold values from -6 to 6
- adj_now: float32 [4, 128, 128, 128], P(None, 'surf', 'depth'), may hold values from -6 to 6
- adj_old: float32 [4, 128, 128, 128], P(None, 'surf', 'depth'), may hold values from -6 to 6
- source: float32 [4, 128, 128, 128], P(None, 'surf', 'depth'), may hold values from -24 to 24
- adj_source: float32 [4, 128, 128, 128], P(None, 'surf', 'depth'), may hold values from -24 to 24
- inv_density: float32 [125, 32768], P(None, ('surf', 'depth')), may hold values from 0.5 to 1.5
- inv_modulus: float32 [125, 32768], P(None, ('surf', 'depth')), may hold values from 0.5 to 1.5
- element_cell: int32 [128, 256], P(('surf', 'depth')), may hold values from 0 to 255, as said below
- send_elem: int32 [128, 4, 256], P(('surf', 'depth')), may hold values from 0 to 255, as said below
- send_brick: int32 [128, 4, 256], P(('surf', 'depth')), may hold values from 0 to 1023, as said below
- send_count: int32 [128, 4], P(('surf', 'depth')), may hold values from 0 to 256, as said below
Outputs:
- wave_next: float32 [4, 128, 128, 128], P(None, 'surf', 'depth')
- adj_next: float32 [4, 128, 128, 128], P(None, 'surf', 'depth')
- brick_kernel: float32 [125, 131072], P(None, ('surf', 'depth'))
Inputs may be any that keep to these rules, and one draw needn't show every extreme that they name: Each row of element_cell is a permutation of the cells of one device. `send_elem`: row t of device k lists in its first send_count[k, t] slots the stored elements of device k whose blocks go to row t's device; over the four rows of a device each of its elements is listed exactly once; other slots hold 0. `send_brick`: in live slots the receiving brick within the receiving device; other slots hold 0. `send_count`: A device's counts sum to 256; rows 1 and 3 of devices with the last surf index, and rows 2 and 3 of devices with the last depth index, are empty; in every draw the device with the last surf and depth index fills row 0 with all 256 slots.
All inputs are finite; a program needn't handle non-finite values.
Results may differ from a plain program's by a relative error of at most 0.0003.
Values sent between devices are 32-bit elements; how exact they have to be, the bound alone decides.
No kernel may reach another device: no remote copies, remote signals or barrier semaphores. Data moves between devices by JAX's collectives and lax.ppermute only.
A program may use at most 128 MiB of HBM per device.

v0:
```python
import math

import jax
import jax.numpy as jnp
import numpy as np
from jax import lax
from jax.experimental import pallas as pl
from jax.experimental.pallas import tpu as pltpu
from jax.sharding import PartitionSpec as P

F32 = jnp.float32
BF16 = jnp.bfloat16
DT = 0.05
NT = (((1,), (1,)), ((), ()))
NROW = 85


def gll():
    x = np.array([-1.0, -math.sqrt(3.0 / 7.0), 0.0, math.sqrt(3.0 / 7.0), 1.0])
    w = np.array([0.1, 49.0 / 90.0, 32.0 / 45.0, 49.0 / 90.0, 0.1])
    eye = np.eye(5)
    diff = x[:, None] - x[None, :] + eye
    prod = np.prod(diff, axis=1)
    deriv = prod[:, None] / prod[None, :] / diff
    inv = np.where(eye > 0.5, 0.0, 1.0 / diff)
    deriv = np.where(eye > 0.5, inv.sum(axis=1)[:, None], deriv)
    return deriv, w


DERIV, WEIGHT = gll()
CUBATURE = (WEIGHT[:, None, None] * WEIGHT[None, :, None] * WEIGHT[None, None, :]).reshape(125, 1)


def spread_table():
    table = np.zeros((4, 128, 5, 4, 32), np.float32)
    for ec in range(4):
        for eb in range(32):
            for r in range(5):
                table[ec, (4 * eb + r) % 128, r, ec, eb] = 1.0
    return table.reshape(512, 640)


def apply_deriv(mat, v):
    e0, e1, e2 = v[0] + v[4], v[1] + v[3], v[2]
    o0, o1 = v[0] - v[4], v[1] - v[3]
    half = lambda i, l: float(0.5 * (mat[i, l] + mat[i, 4 - l]))
    dif = lambda i, l: float(0.5 * (mat[i, l] - mat[i, 4 - l]))
    odd = [half(i, 0) * e0 + half(i, 1) * e1 + float(mat[i, 2]) * e2 for i in (0, 1)]
    even = [dif(i, 0) * o0 + dif(i, 1) * o1 for i in (0, 1, 2)]
    return [even[0] + odd[0], even[1] + odd[1], even[2], even[1] - odd[1], even[0] - odd[0]]


def split2(x):
    hi = x.astype(BF16)
    return hi, (x - hi.astype(F32)).astype(BF16)


def dot2(x, table, dims=(((1,), (0,)), ((), ()))):
    hi, lo = split2(x)
    return lax.dot_general(hi, table, dims, preferred_element_type=F32) + lax.dot_general(
        lo, table, dims, preferred_element_type=F32
    )


def prep_kernel(dens, modu, cell, selem, sbrick, scount, cub, fold, stiff, mass, targ, ms0, ms1, mo):
    place = (lax.broadcasted_iota(jnp.int32, (256, 256), 0) == cell[...]).astype(F32).astype(BF16)
    stiff[0:125, :] = dot2(dens[...], place, NT) * cub[...]
    cells = dot2(modu[...], place, NT) * cub[...]
    mass[...] = jnp.zeros(mass.shape, F32)
    for ea, ms in ((0, ms0), (1, ms1)):
        ms[0:125, :] = cells[:, ea * 128 : ea * 128 + 128]
        rows = jnp.concatenate([ms[pl.ds(r, 25, stride=5), :] for r in range(5)], axis=1)
        mo[...] = dot2(rows, fold[...])
        for p in range(5):
            for ec in range(4):
                at = pl.ds((4 * ea + p) * 17 + 4 * ec, 5)
                mass[at, :] = mass[at, :] + mo[p * 5 : p * 5 + 5, ec * 128 : ec * 128 + 128]
    sub = lax.broadcasted_iota(jnp.int32, (8, 256), 0)
    lane = lax.broadcasted_iota(jnp.int32, (1, 256), 1)
    elem_iota = lax.broadcasted_iota(jnp.int32, (256, 256), 0)
    acc = jnp.zeros((8, 256), F32)
    for t in range(4):
        brick = jnp.where(lane < scount[0, t], sbrick[0, t : t + 1, :] + 1, 0)
        high = lax.shift_right_logical(brick, 5)
        low = brick - high * 32
        rows = jnp.where(sub == t, high, jnp.where(sub == t + 4, low, 0))
        pick = (elem_iota == selem[0, t : t + 1, :]).astype(F32).astype(BF16)
        acc = acc + lax.dot_general(
            rows.astype(F32).astype(BF16), pick, NT, preferred_element_type=F32
        )
    at_cell = lax.dot_general(acc.astype(BF16), place, NT, preferred_element_type=F32)
    targ[0:4, :] = 32.0 * at_cell[0:4] + at_cell[4:8] - 1.0


def element_layer(ea, stiff, spread, fold, kcol, kern, ng, g, lhs, val, prod, frc):
    for p in range(5):
        for c in range(17):
            tile = g[pl.ds(p * 17 + c, 8, stride=NROW), :]
            if c < 16:
                at = (p * 5 + c % 4) * 8
                lhs[at : at + 8, (c // 4) * 128 : (c // 4) * 128 + 128] = tile
            if c % 4 == 0 and c > 0:
                at = (p * 5 + 4) * 8
                lhs[at : at + 8, (c // 4 - 1) * 128 : (c // 4 - 1) * 128 + 128] = tile
    val[...] = dot2(lhs[...], spread[...])

    def tile_at(p, q, r):
        return (slice((p * 5 + q) * 8, (p * 5 + q) * 8 + 8), slice(r * 128, r * 128 + 128))

    lanes = slice(ea * 128, ea * 128 + 128)
    prod[1000:1024, :] = jnp.zeros((24, 128), F32)
    for axis in range(3):
        for i in range(5):
            for j in range(5):
                nodes = [((k, i, j), (i, k, j), (i, j, k))[axis] for k in range(5)]
                grad = apply_deriv(DERIV, [val[tile_at(*n)] for n in nodes])
                flux = []
                for k, n in enumerate(nodes):
                    at = n[0] * 25 + n[1] * 5 + n[2]
                    flux.append(grad[k] * stiff[at : at + 1, lanes])
                force = apply_deriv(DERIV.T, flux)
                for k, n in enumerate(nodes):
                    at = (n[0] * 25 + n[1] * 5 + n[2]) * 8
                    pair = grad[k] * pltpu.roll(grad[k], 4, 0)
                    if axis == 0:
                        prod[at : at + 8, :] = pair
                        frc[tile_at(*n)] = force[k]
                    else:
                        prod[at : at + 8, :] = prod[at : at + 8, :] + pair
                        frc[tile_at(*n)] = frc[tile_at(*n)] + force[k]
    for j in range(16):
        total = sum(prod[pl.ds(j * 64 + t, 8, stride=8), :] for t in range(4))
        kern[j * 8 : j * 8 + 8, :] = total * kcol[j * 8 : j * 8 + 8, :]
    lhs[...] = dot2(frc[...], fold[...])
    for p in range(5):
        for c in range(17):
            parts = []
            if c < 16:
                at = (p * 5 + c % 4) * 8
                parts.append(lhs[at : at + 8, (c // 4) * 128 : (c // 4) * 128 + 128])
            if c % 4 == 0 and c > 0:
                at = (p * 5 + 4) * 8
                parts.append(lhs[at : at + 8, (c // 4 - 1) * 128 : (c // 4 - 1) * 128 + 128])
            ng[pl.ds(p * 17 + c, 8, stride=NROW), :] = sum(parts)


def low_kernel(wave, adj, hc, stiff, spread, fold, kcol, kern, ng, g, lhs, val, prod, frc):
    keep = (lax.axis_index("depth") < lax.axis_size("depth") - 1).astype(F32)
    for x in range(8):
        src = wave if x < 4 else adj
        for p in range(5):
            at = x * NROW + p * 17
            g[at : at + 16, :] = src[x % 4, p]
            g[at + 16 : at + 17, :] = hc[x, p : p + 1, :] * keep
    element_layer(0, stiff, spread, fold, kcol, kern, ng, g, lhs, val, prod, frc)


def high_kernel(
    wave, adj, hc, ha, stiff, spread, fold, kcol, kern_low, ng_low, mass, targ,
    inner, own, buf_s, buf_d, buf_sd, kern, ng, g, lhs, val, prod, frc,
):
    keep_d = (lax.axis_index("depth") < lax.axis_size("depth") - 1).astype(F32)
    keep_s = (lax.axis_index("surf") < lax.axis_size("surf") - 1).astype(F32)
    for x in range(8):
        src = wave if x < 4 else adj
        for p in range(4):
            at = x * NROW + p * 17
            g[at : at + 16, :] = src[x % 4, 4 + p]
            g[at + 16 : at + 17, :] = hc[x, 4 + p : 5 + p, :] * keep_d
        at = x * NROW + 68
        g[at : at + 16, :] = ha[x, 0:16, :] * keep_s
        g[at + 16 : at + 17, :] = ha[x, 16:17, :] * (keep_s * keep_d)
    element_layer(1, stiff, spread, fold, kcol, kern, ng, g, lhs, val, prod, frc)
    for row, buf in ((0, own), (1, buf_s), (2, buf_d), (3, buf_sd)):
        buf[0:128, :] = kern_low[...]
        buf[128:256, :] = kern[...]
        buf[125:126, :] = targ[row : row + 1, 0:128]
        buf[253:254, :] = targ[row : row + 1, 128:256]
    for x in range(8):
        base = x * NROW
        for a in range(8):
            if a < 4:
                rows = ng_low[base + a * 17 : base + a * 17 + 17, :]
            elif a == 4:
                rows = ng_low[base + 68 : base + 85, :] + ng[base : base + 17, :]
            else:
                at = base + (a - 4) * 17
                rows = ng[at : at + 17, :]
            inner[x, a] = rows[0:16]
            buf_d[256 + x * 8 + a : 257 + x * 8 + a, :] = rows[16:17]
        buf_s[256 + x * 16 : 272 + x * 16, :] = ng[base + 68 : base + 84, :]
        buf_sd[256 + x : 257 + x, :] = ng[base + 84 : base + 85, :]
    for a in range(8):
        inner[8, a] = mass[a * 17 : a * 17 + 16, :]
        buf_d[320 + a : 321 + a, :] = mass[a * 17 + 16 : a * 17 + 17, :]
    buf_s[384:400, :] = mass[136:152, :]
    buf_sd[264:265, :] = mass[152:153, :]
    buf_sd[265:272, :] = jnp.zeros((7, 128), F32)


def final_kernel(
    wave, wave_old, adj, adj_old, src, adj_src, inner, own, got_s, got_d, got_sd,
    wave_next, adj_next, bricks,
):
    has_s = lax.axis_index("surf") > 0
    has_d = lax.axis_index("depth") > 0
    keep_s = has_s.astype(F32)
    keep_d = has_d.astype(F32)
    first = lax.broadcasted_iota(jnp.int32, (16, 128), 0) == 0

    def total(ch, a):
        part = inner[ch, a]
        line = got_d[256 + ch * 8 + a : 257 + ch * 8 + a, :] * keep_d
        if a == 0:
            part = part + got_s[256 + ch * 16 : 272 + ch * 16, :] * keep_s
            line = line + got_sd[256 + ch : 257 + ch, :] * (keep_s * keep_d)
        return part + jnp.where(first, line, 0.0)

    for a in range(8):
        scale = (DT * DT) / total(8, a)
        for t in range(4):
            wave_next[t, a] = 2.0 * wave[t, a] - wave_old[t, a] + (src[t, a] - total(t, a)) * scale
            adj_next[t, a] = (
                2.0 * adj[t, a] - adj_old[t, a] + (adj_src[t, a] - total(4 + t, a)) * scale
            )
    rows = lax.broadcasted_iota(jnp.int32, (1024, 128), 0).astype(F32)
    acc = jnp.zeros((128, 1024), F32)
    for buf in (own, got_s, got_d, got_sd):
        for ea in range(2):
            block = buf[ea * 128 : ea * 128 + 128, :]
            hit = jnp.where(rows == block[125:126, :], 1.0, 0.0).astype(BF16)
            acc = acc + dot2(block, hit, NT)
    bricks[...] = acc[0:125, :]


def vmem(*shape):
    return pltpu.VMEM(shape, F32)


def out(*shape):
    return jax.ShapeDtypeStruct(shape, F32)


PARAMS = pltpu.CompilerParams(vmem_limit_bytes=48 * 1024 * 1024)


def ring(x, axis, by):
    size = lax.axis_size(axis)
    return lax.ppermute(x, axis, [(i, (i + by) % size) for i in range(size)])


def diagonal(x):
    ns, nd = lax.axis_size("surf"), lax.axis_size("depth")
    pairs = [
        (s * nd + d, (s + 1) % ns * nd + (d + 1) % nd) for s in range(ns) for d in range(nd)
    ]
    return lax.ppermute(x, ("surf", "depth"), pairs)


def per_device(
    wave_now, wave_old, adj_now, adj_old, source, adj_source,
    inv_density, inv_modulus, element_cell, send_elem, send_brick, send_count,
):
    table = spread_table()
    spread = jnp.asarray(table, BF16)
    fold = jnp.asarray(table.T, BF16)
    cub = jnp.asarray(CUBATURE, F32)
    kcol = jnp.asarray(np.concatenate([-DT * CUBATURE, np.zeros((3, 1))]), F32)

    hc = ring(jnp.concatenate([wave_now[:, :, 0], adj_now[:, :, 0]], 0), "depth", -1)
    plane = jnp.concatenate([wave_now[:, 0], adj_now[:, 0]], 0)
    ha = ring(jnp.concatenate([plane, hc[:, 0:1]], 1), "surf", -1)

    any_ = pl.BlockSpec(memory_space=pltpu.VMEM)
    smem = pl.BlockSpec(memory_space=pltpu.SMEM)
    stiff, mass, targ = pl.pallas_call(
        prep_kernel,
        out_shape=(out(128, 256), out(160, 128), out(8, 256)),
        in_specs=[any_] * 5 + [smem] + [any_] * 2,
        out_specs=(any_, any_, any_),
        scratch_shapes=[vmem(128, 128), vmem(128, 128), vmem(25, 512)],
        compiler_params=PARAMS,
        name="prep",
    )(inv_density, inv_modulus, element_cell, send_elem, send_brick, send_count, cub, fold)

    work = [vmem(8 * NROW, 128), vmem(200, 512), vmem(200, 640), vmem(1024, 128), vmem(200, 640)]
    kern_low, ng_low = pl.pallas_call(
        low_kernel,
        out_shape=(out(128, 128), out(8 * NROW, 128)),
        in_specs=[any_] * 7,
        out_specs=(any_, any_),
        scratch_shapes=work,
        compiler_params=PARAMS,
        name="low",
    )(wave_now, adj_now, hc, stiff, spread, fold, kcol)

    inner, own, buf_s, buf_d, buf_sd = pl.pallas_call(
        high_kernel,
        out_shape=(out(9, 8, 16, 128), out(256, 128), out(400, 128), out(328, 128), out(272, 128)),
        in_specs=[any_] * 12,
        out_specs=(any_,) * 5,
        scratch_shapes=[vmem(128, 128), vmem(8 * NROW, 128)] + work,
        compiler_params=PARAMS,
        name="high",
    )(wave_now, adj_now, hc, ha, stiff, spread, fold, kcol, kern_low, ng_low, mass, targ)

    got_s = ring(buf_s, "surf", 1)
    got_d = ring(buf_d, "depth", 1)
    got_sd = diagonal(buf_sd)

    field = out(*wave_now.shape)
    return pl.pallas_call(
        final_kernel,
        out_shape=(field, field, out(125, 1024)),
        in_specs=[any_] * 11,
        out_specs=(any_,) * 3,
        compiler_params=PARAMS,
        name="final",
    )(
        wave_now, wave_old, adj_now, adj_old, source, adj_source, inner, own, got_s, got_d, got_sd
    )


def solution(mesh):
    field = P(None, "surf", "depth", None)
    both = ("surf", "depth")
    return jax.shard_map(
        per_device,
        mesh=mesh,
        in_specs=(field,) * 6
        + (P(None, both), P(None, both), P(both, None), P(both, None, None), P(both, None, None), P(both, None)),
        out_specs=(field, field, P(None, both)),
        check_vma=False,
    )
```

profile of v0, /device:TPU:1, one launch (start us, length us, event | category | flops | bytes accessed | tf_op | source)
XLA Modules:
  0.0 37.8 jit_solution(15793509991902115823)
XLA Ops:
  0.6 0.9 %slice.15 = f32[4,8,1,128]{3,2,1,0:T(1,128)S(1)} slice(f32[4,8,16,128]{3,2,1,0:T(8,128)} %wave.5), slice={[0:4], [0:8], [0:1], [0:128]} | slice | bytes 32768 | tf_op jit(solution)/shard_map/slice | solution.py:270
  1.5 0.0 copy-start.10
  1.6 1.0 %slice.16 = f32[4,8,1,128]{3,2,1,0:T(1,128)S(1)} slice(f32[4,8,16,128]{3,2,1,0:T(8,128)} %adj.5), slice={[0:4], [0:8], [0:1], [0:128]} | slice | bytes 32768 | tf_op jit(solution)/shard_map/slice | solution.py:270
  2.5 1.4 %collective-permute-start = (f32[8,8,128]{2,1,0:T(8,128)S(1)}, f32[8,8,128]{2,1,0:T(8,128)S(1)}, u32[]{:S(2)}, u32[]{:S(2)}) collective-permute-start(f32[8,8,128]{2,1,0:T(8,128)S(1)} %pad_maximum_fusion.1), channel_id=1, source_target_pairs={{0,7},{1,0},{2,1},{3,2},{4,3},{5,4},{6,5},{7,6},{8,15},{9,8},{10,9... | collective-permute-start | bytes 98312 | tf_op jit(solution)/shard_map/ppermute | solution.py:249
  4.0 0.0 copy-start.3
  4.0 0.8 %slice_bitcast_fusion = (f32[4,16,128]{2,1,0:T(8,128)S(1)}, f32[4,16,128]{2,1,0:T(8,128)S(1)}) fusion(f32[4,8,16,128]{3,2,1,0:T(8,128)} %adj.5, f32[4,8,16,128]{3,2,1,0:T(8,128)} %wave.5), kind=kLoop, calls=%fused_computation.2 | loop fusion | bytes 131072 | tf_op jit(solution)/shard_map/squeeze | solution.py:271
  4.8 1.9 %collective-permute-done.hc = f32[8,8,128]{2,1,0:T(8,128)S(1)} collective-permute-done((f32[8,8,128]{2,1,0:T(8,128)S(1)}, f32[8,8,128]{2,1,0:T(8,128)S(1)}, u32[]{:S(2)}, u32[]{:S(2)}) %collective-permute-start) | collective-permute-done | bytes 32800 | tf_op jit(solution)/shard_map/ppermute | solution.py:249
  6.7 0.0 copy-start.14
  6.8 0.0 copy-start.15
  6.8 0.0 copy-start.16
  6.8 6.3 %collective-permute-start.1 = (f32[8,17,128]{2,1,0:T(8,128)S(1)}, f32[8,17,128]{2,1,0:T(8,128)S(1)}, u32[]{:S(2)}, u32[]{:S(2)}) collective-permute-start(f32[8,17,128]{2,1,0:T(8,128)S(1)} %pad_maximum_fusion), channel_id=1, source_target_pairs={{0,120},{8,0},{16,8},{24,16},{32,24},{40,32},{48,40},{56,48},{64,5... | collective-permute-start | bytes 208904 | tf_op jit(solution)/shard_map/ppermute | solution.py:249
  13.1 0.0 copy-done.10
  13.1 0.0 copy-done.13
  13.1 0.0 copy-done.14
  13.1 0.0 copy-done.15
  13.1 0.0 copy-done.16
  13.1 0.0 copy-start
  13.1 1.1 %copy-done = bf16[640,512]{1,0:T(8,128)(2,1)S(1)} copy-done((bf16[640,512]{1,0:T(8,128)(2,1)S(1)}, bf16[640,512]{1,0:T(8,128)(2,1)}, u32[]{:S(2)}) %copy-start) | copy-done | bytes 655384
  14.2 0.0 copy-start.11
  14.2 0.9 %copy-done.11 = f32[125,256]{1,0:T(8,128)S(1)} copy-done((f32[125,256]{1,0:T(8,128)S(1)}, f32[125,256]{1,0:T(8,128)}, u32[]{:S(2)}) %copy-start.11) | copy-done | bytes 128024
  15.1 0.0 copy-start.12
  15.1 0.8 %copy-done.12 = f32[125,1]{1,0:T(8,128)S(1)} copy-done((f32[125,1]{1,0:T(8,128)S(1)}, f32[125,1]{1,0:T(8,128)}, u32[]{:S(2)}) %copy-start.12) | copy-done | bytes 524
  15.9 0.0 copy-start.1
  15.9 1.7 %prep.1 = (f32[128,256]{1,0:T(8,128)S(1)}, f32[160,128]{1,0:T(8,128)S(1)}, f32[8,256]{1,0:T(8,128)S(1)}) custom-call(f32[125,256]{1,0:T(8,128)S(1)} %copy-done.10, f32[125,256]{1,0:T(8,128)S(1)} %copy-done.11, s32[1,256]{1,0:T(1,128)S(1)} %copy-done.15, s32[1,4,256]{2,1,0:T(4,128)S(1)} %copy-done.13, s32[1,4,256]{2,1,0:T(4,128)S(1)} %copy-done.14, ...), custom_call_target="tpu_custom_call" | custom-call | tf_op jit(solution)/shard_map/prep/pallas_call | solution.py:276
  17.6 0.0 copy-done.3
  17.6 0.0 copy-done.1
  17.7 0.0 copy-done.2
  17.7 0.0 copy-done.9
  17.7 0.0 copy-start.4
  17.7 1.1 %copy-done.4 = bf16[512,640]{1,0:T(8,128)(2,1)S(1)} copy-done((bf16[512,640]{1,0:T(8,128)(2,1)S(1)}, bf16[512,640]{1,0:T(8,128)(2,1)}, u32[]{:S(2)}) %copy-start.4) | copy-done | bytes 655384
  18.8 1.6 %low.1 = (f32[128,128]{1,0:T(8,128)S(1)}, f32[680,128]{1,0:T(8,128)S(1)}) custom-call(f32[4,8,16,128]{3,2,1,0:T(8,128)S(1)} %copy-done.2, f32[4,8,16,128]{3,2,1,0:T(8,128)S(1)} %copy-done.3, f32[8,8,128]{2,1,0:T(8,128)S(1)} %collective-permute-done.hc, f32[128,256]{1,0:T(8,128)S(1)} %get-tuple-element.13.stiff, bf16[512,640]{1,0:T(8,128)(2,1)S(1)} %copy-done.4, ...), custom_call_target="tpu_custom_call" | custom-call | tf_op jit(solution)/shard_map/low/pallas_call | solution.py:287
  20.4 0.0 collective-permute-done.1.ha
  20.4 0.0 copy-start.5
  20.4 0.0 copy-start.6
  20.4 0.0 copy-start.7
  20.4 0.0 copy-start.8
  20.4 1.7 %high.1 = (f32[9,8,16,128]{3,2,1,0:T(8,128)S(1)}, f32[256,128]{1,0:T(8,128)S(1)}, f32[400,128]{1,0:T(8,128)S(1)}, f32[328,128]{1,0:T(8,128)S(1)}, f32[272,128]{1,0:T(8,128)S(1)}) custom-call(f32[4,8,16,128]{3,2,1,0:T(8,128)S(1)} %copy-done.2, f32[4,8,16,128]{3,2,1,0:T(8,128)S(1)} %copy-done.3, f32[8,8,128]{2,1,0:T(8,128)S(1)} %collective-permute-done.hc, ...), custom_call_target="tpu_custom_call" | custom-call | tf_op jit(solution)/shard_map/high/pallas_call | solution.py:297
  22.1 0.1 collective-permute-start.2
  22.2 0.3 collective-permute-start.3
  22.5 0.0 collective-permute-start.4
  22.5 12.9 %collective-permute-done.4.got_sd = f32[272,128]{1,0:T(8,128)S(1)} collective-permute-done((f32[272,128]{1,0:T(8,128)S(1)}, f32[272,128]{1,0:T(8,128)S(1)}, u32[]{:S(2)}, u32[]{:S(2)}) %collective-permute-start.4) | collective-permute-done | bytes 139296 | tf_op jit(solution)/shard_map/ppermute | solution.py:257
  35.4 0.0 collective-permute-done.3.got_d
  35.4 0.0 collective-permute-done.2.got_s
  35.4 0.0 copy-done.5
  35.4 0.0 copy-done.6
  35.5 0.0 copy-done.7
  35.5 0.0 copy-done.8
  35.5 2.3 %final.1 = (f32[4,8,16,128]{3,2,1,0:T(8,128)}, f32[4,8,16,128]{3,2,1,0:T(8,128)}, f32[125,1024]{1,0:T(8,128)}) custom-call(f32[4,8,16,128]{3,2,1,0:T(8,128)S(1)} %copy-done.2, f32[4,8,16,128]{3,2,1,0:T(8,128)S(1)} %copy-done.5, f32[4,8,16,128]{3,2,1,0:T(8,128)S(1)} %copy-done.3, f32[4,8,16,128]{3,2,1,0:T(8,128)S(1)} %copy-done.6, ...), custom_call_target="tpu_custom_call" | custom-call | tf_op jit(solution)/shard_map/final/pallas_call | solution.py:312
  (6 shorter events, 0.0 us)
Async XLA Ops:
  1.5 11.5 %copy-start.10 = (f32[125,256]{1,0:T(8,128)S(1)}, f32[125,256]{1,0:T(8,128)}, u32[]{:S(2)}) copy-start(f32[125,256]{1,0:T(8,128)} %dens.1) | copy-start | bytes 384004
  2.5 4.2 %collective-permute-start = (f32[8,8,128]{2,1,0:T(8,128)S(1)}, f32[8,8,128]{2,1,0:T(8,128)S(1)}, u32[]{:S(2)}, u32[]{:S(2)}) collective-permute-start(f32[8,8,128]{2,1,0:T(8,128)S(1)} %pad_maximum_fusion.1), channel_id=1, source_target_pairs={{0,7},{1,0},{2,1},{3,2},{4,3},{5,4},{6,5},{7,6},{8,15},{9,8},{10,9... | collective-permute-start | bytes 98312 | tf_op jit(solution)/shard_map/ppermute | solution.py:249
  4.0 13.7 %copy-start.3 = (f32[4,8,16,128]{3,2,1,0:T(8,128)S(1)}, f32[4,8,16,128]{3,2,1,0:T(8,128)}, u32[]{:S(2)}) copy-start(f32[4,8,16,128]{3,2,1,0:T(8,128)} %adj.5) | copy-start | bytes 786436
  6.7 6.3 %copy-start.13 = (s32[1,4,256]{2,1,0:T(4,128)S(1)}, s32[1,4,256]{2,1,0:T(4,128)}, u32[]{:S(2)}) copy-start(s32[1,4,256]{2,1,0:T(4,128)} %selem.1) | copy-start | bytes 12292
  6.7 6.3 %copy-start.14 = (s32[1,4,256]{2,1,0:T(4,128)S(1)}, s32[1,4,256]{2,1,0:T(4,128)}, u32[]{:S(2)}) copy-start(s32[1,4,256]{2,1,0:T(4,128)} %sbrick.1) | copy-start | bytes 12292
  6.8 6.3 %copy-start.15 = (s32[1,256]{1,0:T(1,128)S(1)}, s32[1,256]{1,0:T(1,128)}, u32[]{:S(2)}) copy-start(s32[1,256]{1,0:T(1,128)} %cell.1) | copy-start | bytes 3076
  6.8 6.3 %copy-start.16 = (s32[1,4]{1,0:T(1,128)S(1)}, s32[1,4]{1,0:T(1,128)}, u32[]{:S(2)}) copy-start(s32[1,4]{1,0:T(1,128)} %scount.1) | copy-start | bytes 52
  6.8 13.6 %collective-permute-start.1 = (f32[8,17,128]{2,1,0:T(8,128)S(1)}, f32[8,17,128]{2,1,0:T(8,128)S(1)}, u32[]{:S(2)}, u32[]{:S(2)}) collective-permute-start(f32[8,17,128]{2,1,0:T(8,128)S(1)} %pad_maximum_fusion), channel_id=1, source_target_pairs={{0,120},{8,0},{16,8},{24,16},{32,24},{40,32},{48,40},{56,48},{64,5... | collective-permute-start | bytes 208904 | tf_op jit(solution)/shard_map/ppermute | solution.py:249
  13.1 1.1 %copy-start = (bf16[640,512]{1,0:T(8,128)(2,1)S(1)}, bf16[640,512]{1,0:T(8,128)(2,1)}, u32[]{:S(2)}) copy-start(bf16[640,512]{1,0:T(8,128)(2,1)} %constant.9.clone.fold) | copy-start | bytes 1966084
  14.2 0.9 %copy-start.11 = (f32[125,256]{1,0:T(8,128)S(1)}, f32[125,256]{1,0:T(8,128)}, u32[]{:S(2)}) copy-start(f32[125,256]{1,0:T(8,128)} %modu.1) | copy-start | bytes 384004
  15.1 0.8 %copy-start.12 = (f32[125,1]{1,0:T(8,128)S(1)}, f32[125,1]{1,0:T(8,128)}, u32[]{:S(2)}) copy-start(f32[125,1]{1,0:T(8,128)} %constant.10.clone.cub) | copy-start | bytes 1504
  15.9 1.7 %copy-start.1 = (bf16[640,512]{1,0:T(8,128)(2,1)S(1)}, bf16[640,512]{1,0:T(8,128)(2,1)}, u32[]{:S(2)}) copy-start(bf16[640,512]{1,0:T(8,128)(2,1)} %constant.9.clone.fold) | copy-start | bytes 1966084
  15.9 1.7 %copy-start.2 = (f32[4,8,16,128]{3,2,1,0:T(8,128)S(1)}, f32[4,8,16,128]{3,2,1,0:T(8,128)}, u32[]{:S(2)}) copy-start(f32[4,8,16,128]{3,2,1,0:T(8,128)} %wave.5) | copy-start | bytes 786436
  15.9 1.7 %copy-start.9 = (f32[128,1]{1,0:T(8,128)S(1)}, f32[128,1]{1,0:T(8,128)}, u32[]{:S(2)}) copy-start(f32[128,1]{1,0:T(8,128)} %constant.11.clone.kcol) | copy-start | bytes 1540
  17.7 1.1 %copy-start.4 = (bf16[512,640]{1,0:T(8,128)(2,1)S(1)}, bf16[512,640]{1,0:T(8,128)(2,1)}, u32[]{:S(2)}) copy-start(bf16[512,640]{1,0:T(8,128)(2,1)} %constant.8.clone.spread) | copy-start | bytes 1966084
  20.4 15.0 %copy-start.5 = (f32[4,8,16,128]{3,2,1,0:T(8,128)S(1)}, f32[4,8,16,128]{3,2,1,0:T(8,128)}, u32[]{:S(2)}) copy-start(f32[4,8,16,128]{3,2,1,0:T(8,128)} %wave_old.1) | copy-start | bytes 786436
  20.4 15.0 %copy-start.6 = (f32[4,8,16,128]{3,2,1,0:T(8,128)S(1)}, f32[4,8,16,128]{3,2,1,0:T(8,128)}, u32[]{:S(2)}) copy-start(f32[4,8,16,128]{3,2,1,0:T(8,128)} %adj_old.1) | copy-start | bytes 786436
  20.4 15.0 %copy-start.7 = (f32[4,8,16,128]{3,2,1,0:T(8,128)S(1)}, f32[4,8,16,128]{3,2,1,0:T(8,128)}, u32[]{:S(2)}) copy-start(f32[4,8,16,128]{3,2,1,0:T(8,128)} %src.1) | copy-start | bytes 786436
  20.4 15.0 %copy-start.8 = (f32[4,8,16,128]{3,2,1,0:T(8,128)S(1)}, f32[4,8,16,128]{3,2,1,0:T(8,128)}, u32[]{:S(2)}) copy-start(f32[4,8,16,128]{3,2,1,0:T(8,128)} %adj_src.1) | copy-start | bytes 786436
  22.1 13.3 %collective-permute-start.2 = (f32[400,128]{1,0:T(8,128)S(1)}, f32[400,128]{1,0:T(8,128)S(1)}, u32[]{:S(2)}, u32[]{:S(2)}) collective-permute-start(f32[400,128]{1,0:T(8,128)S(1)} %get-tuple-element.20), channel_id=1, source_target_pairs={{0,8},{8,16},{16,24},{24,32},{32,40},{40,48},{48,56},{56,64},{64,7... | collective-permute-start | bytes 614408 | tf_op jit(solution)/shard_map/ppermute | solution.py:249
  22.2 13.2 %collective-permute-start.3 = (f32[328,128]{1,0:T(8,128)S(1)}, f32[328,128]{1,0:T(8,128)S(1)}, u32[]{:S(2)}, u32[]{:S(2)}) collective-permute-start(f32[328,128]{1,0:T(8,128)S(1)} %get-tuple-element.21), channel_id=1, source_target_pairs={{0,1},{1,2},{2,3},{3,4},{4,5},{5,6},{6,7},{7,0},{8,9},{9,10},{10,1... | collective-permute-start | bytes 503816 | tf_op jit(solution)/shard_map/ppermute | solution.py:249
  22.5 12.9 %collective-permute-start.4 = (f32[272,128]{1,0:T(8,128)S(1)}, f32[272,128]{1,0:T(8,128)S(1)}, u32[]{:S(2)}, u32[]{:S(2)}) collective-permute-start(f32[272,128]{1,0:T(8,128)S(1)} %get-tuple-element.22), channel_id=1, source_target_pairs={{0,9},{1,10},{2,11},{3,12},{4,13},{5,14},{6,15},{7,8},{8,17},{9,18... | collective-permute-start | bytes 417800 | tf_op jit(solution)/shard_map/ppermute | solution.py:257
where the time goes:
time: 38.1 us; the launch traced here: 37.8 us
  waiting for transfers between devices  14.9 us (39%)
  starting transfers between devices  8.07 us (21%)
  Pallas kernels  7.24 us (19%)
  local copies, waits for them, and re-layouts  6.71 us (18%)
  between operations  0.83 us (2%)
    ppermute x1, waiting for transfers between devices, diagonal(): return lax.ppermute(x, ('surf', 'depth'), pairs)  12.9 us
    ppermute x4, starting transfers between devices, ring(): return lax.ppermute(x, axis, [(i, (i + by) % size) for i in range(size)])  8.07 us
    unnamed x34, local copies, waits for them, and re-layouts  4 us
    pallas_call x1, Pallas kernels, per_device(): pl.pallas_call(final_kernel, out_shape=(field, field, out(125, 1024)), in...  2.28 us
    ppermute x4, waiting for transfers between devices, ring(): return lax.ppermute(x, axis, [(i, (i + by) % size) for i in range(size)])  1.95 us
    pallas_call x1, Pallas kernels, per_device(): pl.pallas_call(prep_kernel, out_shape=(out(128, 256), out(160, 128), out(...  1.69 us
    pallas_call x1, Pallas kernels, per_device(): pl.pallas_call(high_kernel, out_shape=(out(9, 8, 16, 128), out(256, 128),...  1.66 us
    pallas_call x1, Pallas kernels, per_device(): pl.pallas_call(low_kernel, out_shape=(out(128, 128), out(8 * NROW, 128)),...  1.61 us
  transfers between devices with their start and end apart: 5, of which 2 were waited for; matrix products, arithmetic and copies ran while one was open for 2% of the time, Pallas kernels for 9%

commit v1 on v0

v1 whole, which is shorter than its diff:
```python
import math

import jax
import jax.numpy as jnp
import numpy as np
from jax import lax
from jax.experimental import pallas as pl
from jax.experimental.pallas import tpu as pltpu
from jax.sharding import PartitionSpec as P

F32 = jnp.float32
BF16 = jnp.bfloat16
DT = 0.05
NT = (((1,), (1,)), ((), ()))
NROW = 85
PLANE = 128


def gll():
    x = np.array([-1.0, -math.sqrt(3.0 / 7.0), 0.0, math.sqrt(3.0 / 7.0), 1.0])
    w = np.array([0.1, 49.0 / 90.0, 32.0 / 45.0, 49.0 / 90.0, 0.1])
    eye = np.eye(5)
    diff = x[:, None] - x[None, :] + eye
    prod = np.prod(diff, axis=1)
    deriv = prod[:, None] / prod[None, :] / diff
    inv = np.where(eye > 0.5, 0.0, 1.0 / diff)
    deriv = np.where(eye > 0.5, inv.sum(axis=1)[:, None], deriv)
    return deriv, w


DERIV, WEIGHT = gll()


def apply_deriv(mat, v):
    e0, e1, e2 = v[0] + v[4], v[1] + v[3], v[2]
    o0, o1 = v[0] - v[4], v[1] - v[3]
    half = lambda i, l: float(0.5 * (mat[i, l] + mat[i, 4 - l]))
    dif = lambda i, l: float(0.5 * (mat[i, l] - mat[i, 4 - l]))
    odd = [half(i, 0) * e0 + half(i, 1) * e1 + float(mat[i, 2]) * e2 for i in (0, 1)]
    even = [dif(i, 0) * o0 + dif(i, 1) * o1 for i in (0, 1, 2)]
    return [even[0] + odd[0], even[1] + odd[1], even[2], even[1] - odd[1], even[0] - odd[0]]


def split2(x):
    hi = x.astype(BF16)
    return hi, (x - hi.astype(F32)).astype(BF16)


def dot2(x, table, dims=(((1,), (0,)), ((), ()))):
    hi, lo = split2(x)
    return lax.dot_general(hi, table, dims, preferred_element_type=F32) + lax.dot_general(
        lo, table, dims, preferred_element_type=F32
    )


def pack_kernel(wave, adj, line, plane, sem):
    copies = []
    for k, src in enumerate((wave, adj)):
        to = pl.ds(4 * k, 4)
        copies.append(pltpu.make_async_copy(src.at[:, :, 0, :], line.at[to], sem.at[2 * k]))
        copies.append(pltpu.make_async_copy(src.at[:, 0], plane.at[to], sem.at[2 * k + 1]))
    for c in copies:
        c.start()
    for c in copies:
        c.wait()


def prep_kernel(
    dens_hbm, modu_hbm, cell_hbm, selem_hbm, sbrick_hbm, scount, stiff, mass, targ, spread, fold, wcol,
    dens, modu, cell, selem, sbrick, sem, ms0, ms1, mo,
):
    pairs = (
        (dens_hbm, dens), (modu_hbm, modu), (cell_hbm, cell), (selem_hbm, selem), (sbrick_hbm, sbrick)
    )
    copies = [pltpu.make_async_copy(a, b, sem.at[k]) for k, (a, b) in enumerate(pairs)]
    for c in copies:
        c.start()
    sub = lax.broadcasted_iota(jnp.int32, (128, 128), 0)
    lane = lax.broadcasted_iota(jnp.int32, (128, 128), 1)
    fold[...] = jnp.zeros(fold.shape, BF16)
    for r in range(5):
        node = (4 * (lane & 31) + r) & 127
        hit = sub == node
        for ec in range(4):
            spread[ec * 128 : ec * 128 + 128, r * 128 : r * 128 + 128] = jnp.where(
                hit & ((lane >> 5) == ec), 1.0, 0.0
            ).astype(BF16)
        back = jnp.where(lane == ((4 * (sub & 31) + r) & 127), 1.0, 0.0).astype(BF16)
        for ec in range(4):
            rows = slice(r * 128 + ec * 32, r * 128 + ec * 32 + 32)
            fold[rows, ec * 128 : ec * 128 + 128] = back[ec * 32 : ec * 32 + 32]

    def weight(i):
        edge = float(WEIGHT[0])
        return jnp.where(
            i == 2, float(WEIGHT[2]), jnp.where((i == 0) | (i == 4), edge, float(WEIGHT[1]))
        )

    p = (sub >= 25).astype(jnp.int32) + (sub >= 50) + (sub >= 75) + (sub >= 100) + (sub >= 125)
    rest = sub - 25 * p
    q = (rest >= 5).astype(jnp.int32) + (rest >= 10) + (rest >= 15) + (rest >= 20)
    cub = weight(p) * weight(q) * weight(rest - 5 * q)
    wcol[...] = cub * -DT
    for c in copies:
        c.wait()
    both = jnp.concatenate([cub[0:125], cub[0:125]], axis=1)
    place = (lax.broadcasted_iota(jnp.int32, (256, 256), 0) == cell[...]).astype(F32).astype(BF16)
    stiff[0:125, :] = dot2(dens[...], place, NT) * both
    cells = dot2(modu[...], place, NT) * both
    mass[...] = jnp.zeros(mass.shape, F32)
    for ea, ms in ((0, ms0), (1, ms1)):
        ms[0:125, :] = cells[:, ea * 128 : ea * 128 + 128]
        rows = jnp.concatenate([ms[pl.ds(r, 25, stride=5), :] for r in range(5)], axis=1)
        mo[...] = dot2(rows, fold[...])
        for p in range(5):
            for ec in range(4):
                at = pl.ds((4 * ea + p) * 17 + 4 * ec, 5)
                mass[at, :] = mass[at, :] + mo[p * 5 : p * 5 + 5, ec * 128 : ec * 128 + 128]
    sub = lax.broadcasted_iota(jnp.int32, (8, 256), 0)
    lane = lax.broadcasted_iota(jnp.int32, (1, 256), 1)
    elem_iota = lax.broadcasted_iota(jnp.int32, (256, 256), 0)
    acc = jnp.zeros((8, 256), F32)
    for t in range(4):
        brick = jnp.where(lane < scount[0, t], sbrick[0, t : t + 1, :] + 1, 0)
        high = lax.shift_right_logical(brick, 5)
        low = brick - high * 32
        rows = jnp.where(sub == t, high, jnp.where(sub == t + 4, low, 0))
        pick = (elem_iota == selem[0, t : t + 1, :]).astype(F32).astype(BF16)
        acc = acc + lax.dot_general(
            rows.astype(F32).astype(BF16), pick, NT, preferred_element_type=F32
        )
    at_cell = lax.dot_general(acc.astype(BF16), place, NT, preferred_element_type=F32)
    targ[0:4, :] = 32.0 * at_cell[0:4] + at_cell[4:8] - 1.0


def load_plane(g, step, p, lhs, row):
    for c in range(17):
        tile = g[pl.ds(p * 17 + c, 8, stride=step), :]
        if c < 16:
            at = row + c % 4 * 8
            lhs[at : at + 8, c // 4 * 128 : c // 4 * 128 + 128] = tile
        if c % 4 == 0 and c > 0:
            lhs[row + 32 : row + 40, (c // 4 - 1) * 128 : c // 4 * 128] = tile


def node_tile(p, q, r):
    return (slice((p * 5 + q) * 8, (p * 5 + q) * 8 + 8), slice(r * 128, r * 128 + 128))


def node_rows(p, q, r):
    at = (p * 25 + q * 5 + r) * 8
    return slice(at, at + 8)


def line_terms(ea, nodes, values, stiff):
    lanes = slice(ea * 128, ea * 128 + 128)
    grad = apply_deriv(DERIV, values)
    flux = []
    for k, (p, q, r) in enumerate(nodes):
        at = p * 25 + q * 5 + r
        flux.append(grad[k] * stiff[at : at + 1, lanes])
    return [g * pltpu.roll(g, 4, 0) for g in grad], apply_deriv(DERIV.T, flux)


def inside_plane(ea, p, val, at, stiff, prod, frc):
    for i in range(5):
        nodes = [(p, k, i) for k in range(5)]
        pair, force = line_terms(ea, nodes, [val[node_tile(at, k, i)] for k in range(5)], stiff)
        for k, n in enumerate(nodes):
            prod[node_rows(*n), :] = pair[k]
            frc[node_tile(*n)] = force[k]
    for i in range(5):
        nodes = [(p, i, k) for k in range(5)]
        pair, force = line_terms(ea, nodes, [val[node_tile(at, i, k)] for k in range(5)], stiff)
        for k, n in enumerate(nodes):
            prod[node_rows(*n), :] = prod[node_rows(*n), :] + pair[k]
            frc[node_tile(*n)] = frc[node_tile(*n)] + force[k]


def across_planes(ea, val, last, stiff, prod_in, frc_in, prod, frc):
    for q in range(5):
        for r in range(5):
            nodes = [(k, q, r) for k in range(5)]
            values = [val[node_tile(k, q, r)] for k in range(4)] + [last(q, r)]
            pair, force = line_terms(ea, nodes, values, stiff)
            for k, n in enumerate(nodes):
                old_p, old_f = (prod_in, frc_in) if k < 4 else (prod, frc)
                prod[node_rows(*n), :] = old_p[node_rows(*n), :] + pair[k]
                frc[node_tile(*n)] = old_f[node_tile(*n)] + force[k]


def finish_layer(prod, frc, lhs, fold, wcol, kern, ng):
    for j in range(16):
        count = 8 if j < 15 else 5
        total = sum(prod[pl.ds(j * 64 + t, count, stride=8), :] for t in range(4))
        kern[j * 8 : j * 8 + count, :] = total * wcol[j * 8 : j * 8 + count, :]
    kern[125:128, :] = jnp.zeros((3, 128), F32)
    lhs[...] = dot2(frc[...], fold[...])
    for p in range(5):
        for c in range(17):
            parts = []
            if c < 16:
                at = (p * 5 + c % 4) * 8
                parts.append(lhs[at : at + 8, c // 4 * 128 : c // 4 * 128 + 128])
            if c % 4 == 0 and c > 0:
                at = (p * 5 + 4) * 8
                parts.append(lhs[at : at + 8, (c // 4 - 1) * 128 : c // 4 * 128])
            ng[pl.ds(p * 17 + c, 8, stride=NROW), :] = sum(parts)


def early_kernel(
    wave, adj, hc, stiff, spread, fold, wcol, kern, ng, val_up, prod_up, frc_up, g, lhs, val, prod, frc
):
    keep = (lax.axis_index("depth") < lax.axis_size("depth") - 1).astype(F32)
    for ea, planes in ((0, 5), (1, 4)):
        for x in range(8):
            src = wave if x < 4 else adj
            for p in range(planes):
                at = x * NROW + p * 17
                row = x % 4 * PLANE + (4 * ea + p) * 16
                g[at : at + 16, :] = src[row : row + 16, :]
                g[at + 16 : at + 17, :] = hc[x, 4 * ea + p : 4 * ea + p + 1, :] * keep
        for p in range(planes):
            load_plane(g, NROW, p, lhs, p * 40)
        if ea == 0:
            val[...] = dot2(lhs[...], spread[...])
            for p in range(5):
                inside_plane(0, p, val, p, stiff, prod, frc)
            across_planes(0, val, lambda q, r: val[node_tile(4, q, r)], stiff, prod, frc, prod, frc)
            finish_layer(prod, frc, lhs, fold, wcol, kern, ng)
        else:
            val_up[...] = dot2(lhs[0:160, :], spread[...])
            for p in range(4):
                inside_plane(1, p, val_up, p, stiff, prod_up, frc_up)


def late_kernel(
    ha, stiff, spread, fold, wcol, kern_low, ng_low, mass, targ, val_up, prod_up, frc_up,
    inner, own, buf_s, buf_d, buf_sd, kern, ng, g, lhs, val, prod, frc,
):
    keep_d = (lax.axis_index("depth") < lax.axis_size("depth") - 1).astype(F32)
    keep_s = (lax.axis_index("surf") < lax.axis_size("surf") - 1).astype(F32)
    for x in range(8):
        g[x * 17 : x * 17 + 16, :] = ha[x, 0:16, :] * keep_s
        g[x * 17 + 16 : x * 17 + 17, :] = ha[x, 16:17, :] * (keep_s * keep_d)
    load_plane(g, 17, 0, lhs, 0)
    val[...] = dot2(lhs[0:40, :], spread[...])
    inside_plane(1, 4, val, 0, stiff, prod, frc)
    across_planes(1, val_up, lambda q, r: val[node_tile(0, q, r)], stiff, prod_up, frc_up, prod, frc)
    finish_layer(prod, frc, lhs, fold, wcol, kern, ng)
    for row, buf in ((0, own), (1, buf_s), (2, buf_d), (3, buf_sd)):
        buf[0:128, :] = kern_low[...]
        buf[128:256, :] = kern[...]
        buf[125:126, :] = targ[row : row + 1, 0:128]
        buf[253:254, :] = targ[row : row + 1, 128:256]
    for x in range(8):
        base = x * NROW
        for a in range(8):
            if a < 4:
                rows = ng_low[base + a * 17 : base + a * 17 + 17, :]
            elif a == 4:
                rows = ng_low[base + 68 : base + 85, :] + ng[base : base + 17, :]
            else:
                at = base + (a - 4) * 17
                rows = ng[at : at + 17, :]
            inner[x, a] = rows[0:16]
            buf_d[256 + x * 8 + a : 257 + x * 8 + a, :] = rows[16:17]
        buf_s[256 + x * 16 : 272 + x * 16, :] = ng[base + 68 : base + 84, :]
        buf_sd[256 + x : 257 + x, :] = ng[base + 84 : base + 85, :]
    for a in range(8):
        inner[8, a] = mass[a * 17 : a * 17 + 16, :]
        buf_d[320 + a : 321 + a, :] = mass[a * 17 + 16 : a * 17 + 17, :]
    buf_s[384:400, :] = mass[136:152, :]
    buf_sd[264:265, :] = mass[152:153, :]
    buf_sd[265:272, :] = jnp.zeros((7, 128), F32)


def add_bricks(acc, buf, rows):
    for ea in range(2):
        block = buf[ea * 128 : ea * 128 + 128, :]
        hit = jnp.where(rows == block[125:126, :], 1.0, 0.0).astype(BF16)
        term = dot2(block, hit, NT)
        acc = term if acc is None else acc + term
    return acc


def own_kernel(own, part):
    rows = lax.broadcasted_iota(jnp.int32, (1024, 128), 0).astype(F32)
    part[...] = add_bricks(None, own, rows)


def final_kernel(
    wave, wave_old, adj, adj_old, src, adj_src, inner, part, got_s, got_d, got_sd,
    wave_next, adj_next, bricks, wave_buf, adj_buf, brick_buf, sem,
):
    has_s = lax.axis_index("surf") > 0
    has_d = lax.axis_index("depth") > 0
    keep_s = has_s.astype(F32)
    keep_d = has_d.astype(F32)
    first = lax.broadcasted_iota(jnp.int32, (16, 128), 0) == 0

    def total(ch, a):
        part = inner[ch, a]
        line = got_d[256 + ch * 8 + a : 257 + ch * 8 + a, :] * keep_d
        if a == 0:
            part = part + got_s[256 + ch * 16 : 272 + ch * 16, :] * keep_s
            line = line + got_sd[256 + ch : 257 + ch, :] * (keep_s * keep_d)
        return part + jnp.where(first, line, 0.0)

    for a in range(8):
        scale = (DT * DT) / total(8, a)
        for t in range(4):
            at = slice(t * PLANE + a * 16, t * PLANE + a * 16 + 16)
            wave_buf[at, :] = 2.0 * wave[at, :] - wave_old[at, :] + (src[at, :] - total(t, a)) * scale
            adj_buf[at, :] = (
                2.0 * adj[at, :] - adj_old[at, :] + (adj_src[at, :] - total(4 + t, a)) * scale
            )
    copies = [
        pltpu.make_async_copy(wave_buf, wave_next, sem.at[0]),
        pltpu.make_async_copy(adj_buf, adj_next, sem.at[1]),
    ]
    for c in copies:
        c.start()
    for k in range(2):
        cols = slice(k * 512, k * 512 + 512)
        rows = lax.broadcasted_iota(jnp.int32, (512, 128), 0).astype(F32) + float(k * 512)
        acc = part[:, cols]
        for buf in (got_s, got_d, got_sd):
            acc = add_bricks(acc, buf, rows)
        brick_buf[:, cols] = acc[0:125, :]
        copy = pltpu.make_async_copy(brick_buf.at[:, cols], bricks.at[:, cols], sem.at[2 + k])
        copy.start()
        copies.append(copy)
    for c in copies:
        c.wait()


def vmem(*shape):
    return pltpu.VMEM(shape, F32)


def out(*shape, dtype=F32):
    return jax.ShapeDtypeStruct(shape, dtype)


def send(x, ds, dd, wrap_s, wrap_d):
    ns, nd = lax.axis_size("surf"), lax.axis_size("depth")
    pairs = [
        (s * nd + d, (s + ds) % ns * nd + (d + dd) % nd)
        for s in range(ns)
        for d in range(nd)
        if (wrap_s or 0 <= s + ds < ns) and (wrap_d or 0 <= d + dd < nd)
    ]
    return lax.ppermute(x, ("surf", "depth"), pairs)


def call(kernel, name, ins, outs, scratch=(), specs=None, out_space=pltpu.VMEM):
    here = pl.BlockSpec(memory_space=pltpu.VMEM)
    return pl.pallas_call(
        kernel,
        out_shape=tuple(outs),
        in_specs=specs or [here] * len(ins),
        out_specs=tuple(pl.BlockSpec(memory_space=out_space) for _ in outs),
        scratch_shapes=list(scratch),
        compiler_params=pltpu.CompilerParams(vmem_limit_bytes=48 * 1024 * 1024),
        name=name,
    )(*ins)


def in_hbm(x):
    return pltpu.with_memory_space_constraint(x, pltpu.HBM)


def per_device(
    wave_now, wave_old, adj_now, adj_old, source, adj_source,
    inv_density, inv_modulus, element_cell, send_elem, send_brick, send_count,
):
    shape = wave_now.shape
    wave, wave_old, adj, adj_old, source, adj_source = (
        x.reshape(4 * PLANE, 128)
        for x in (wave_now, wave_old, adj_now, adj_old, source, adj_source)
    )
    there = pl.BlockSpec(memory_space=pltpu.HBM)
    line, plane = call(
        pack_kernel, "pack", [in_hbm(x) for x in (wave_now, adj_now)], (out(8, 8, 128), out(8, 16, 128)),
        [pltpu.SemaphoreType.DMA((4,))], [there] * 2,
    )
    hc = send(line, 0, -1, True, True)
    prep = call(
        prep_kernel,
        "prep",
        [in_hbm(x) for x in (inv_density, inv_modulus, element_cell, send_elem, send_brick)]
        + [send_count],
        (out(128, 256), out(160, 128), out(8, 256), out(512, 640, dtype=BF16),
         out(640, 512, dtype=BF16), out(128, 128)),
        [vmem(125, 256), vmem(125, 256), pltpu.VMEM((1, 256), jnp.int32),
         pltpu.VMEM((1, 4, 256), jnp.int32), pltpu.VMEM((1, 4, 256), jnp.int32),
         pltpu.SemaphoreType.DMA((5,)), vmem(128, 128), vmem(128, 128), vmem(25, 512)],
        [there] * 5 + [pl.BlockSpec(memory_space=pltpu.SMEM)],
    )
    hc, plane, prep = lax.optimization_barrier((hc, plane, tuple(prep)))
    stiff, mass, targ, spread, fold, wcol = prep
    ha = send(jnp.concatenate([plane, hc[:, 0:1]], 1), -1, 0, True, True)

    kern_low, ng_low, val_up, prod_up, frc_up = call(
        early_kernel,
        "early",
        (wave, adj, hc, stiff, spread, fold, wcol),
        (out(128, 128), out(8 * NROW, 128), out(160, 640), out(800, 128), out(160, 640)),
        [vmem(8 * NROW, 128), vmem(200, 512), vmem(200, 640), vmem(1000, 128), vmem(200, 640)],
    )
    inner, own, buf_s, buf_d, buf_sd = call(
        late_kernel,
        "late",
        (ha, stiff, spread, fold, wcol, kern_low, ng_low, mass, targ, val_up, prod_up, frc_up),
        (out(9, 8, 16, 128), out(256, 128), out(400, 128), out(328, 128), out(272, 128)),
        [vmem(128, 128), vmem(8 * NROW, 128), vmem(8 * 17, 128), vmem(200, 512), vmem(40, 640),
         vmem(1000, 128), vmem(200, 640)],
    )
    got_s = send(buf_s, 1, 0, False, True)
    got_d = send(buf_d, 0, 1, True, True)
    got_sd = send(buf_sd, 1, 1, False, False)
    (part,) = call(own_kernel, "own", (own,), (out(128, 1024),))
    wave_next, adj_next, bricks = call(
        final_kernel,
        "final",
        (wave, wave_old, adj, adj_old, source, adj_source, inner, part, got_s, got_d, got_sd),
        (out(4 * PLANE, 128), out(4 * PLANE, 128), out(125, 1024)),
        [vmem(4 * PLANE, 128), vmem(4 * PLANE, 128), vmem(125, 1024), pltpu.SemaphoreType.DMA((4,))],
        out_space=pl.ANY,
    )
    return wave_next.reshape(shape), adj_next.reshape(shape), bricks


def solution(mesh):
    field = P(None, "surf", "depth", None)
    both = ("surf", "depth")
    return jax.shard_map(
        per_device,
        mesh=mesh,
        in_specs=(field,) * 6
        + (P(None, both), P(None, both), P(both, None), P(both, None, None), P(both, None, None), P(both, None)),
        out_specs=(field, field, P(None, both)),
        check_vma=False,
    )
```

time: 38.1 us -> 30 us (0.79)
  the two profiles are of different devices: /device:TPU:1 before, /device:TPU:31 now
where the time goes in v1:
time: 30 us; the launch traced here: 29.8 us
  waiting for transfers between devices  10.1 us (34%)
  Pallas kernels  9.5 us (32%)
  starting transfers between devices  9.37 us (31%)
  between operations  0.78 us (3%)
    ppermute x5, waiting for transfers between devices, send(): return lax.ppermute(x, ('surf', 'depth'), pairs)  10.1 us
    pallas_call x6, Pallas kernels, call(): pl.pallas_call(kernel, out_shape=tuple(outs), in_specs=specs or [here] *...  9.5 us
    ppermute x5, starting transfers between devices, send(): return lax.ppermute(x, ('surf', 'depth'), pairs)  9.37 us
  transfers between devices with their start and end apart: 5, of which 2 were waited for; matrix products, arithmetic and copies ran while one was open for 0% of the time, Pallas kernels for 18%

profile of v1, /device:TPU:31, one launch (start us, length us, event | category | flops | bytes accessed | tf_op | source)
XLA Modules:
  0.0 29.8 jit_solution(6621069254335566329)
XLA Ops:
  0.6 0.0 copy-start.6
  0.6 0.0 copy-start.1
  0.7 0.9 %pack.1 = (f32[8,8,128]{2,1,0:T(8,128)S(1)}, f32[8,16,128]{2,1,0:T(8,128)S(1)}) custom-call(f32[4,8,16,128]{3,2,1,0:T(8,128)} %wave.1, f32[4,8,16,128]{3,2,1,0:T(8,128)} %adj.1), custom_call_target="tpu_custom_call" | custom-call | tf_op jit(solution)/shard_map/pack/pallas_call | solution.py:359
  1.6 0.0 copy-start
  1.6 0.7 %collective-permute-start = (f32[8,8,128]{2,1,0:T(8,128)S(1)}, f32[8,8,128]{2,1,0:T(8,128)S(1)}, u32[]{:S(2)}, u32[]{:S(2)}) collective-permute-start(f32[8,8,128]{2,1,0:T(8,128)S(1)} %get-tuple-element.32), channel_id=1, source_target_pairs={{0,7},{1,0},{2,1},{3,2},{4,3},{5,4},{6,5},{7,6},{8,15},{9,8},{10,9... | collective-permute-start | bytes 98312 | tf_op jit(solution)/shard_map/ppermute | solution.py:354
  2.3 0.0 copy-done.6
  2.3 2.7 %prep.1 = (f32[128,256]{1,0:T(8,128)S(1)}, f32[160,128]{1,0:T(8,128)S(1)}, f32[8,256]{1,0:T(8,128)S(1)}, bf16[512,640]{1,0:T(8,128)(2,1)S(1)}, bf16[640,512]{1,0:T(8,128)(2,1)S(1)}, /*index=5*/f32[128,128]{1,0:T(8,128)S(1)}) custom-call(f32[125,256]{1,0:T(8,128)} %dens_hbm.1, f32[125,256]{1,0:T(8,128)} %modu_hbm.1, s32[1,256]{1,0:T(1,128)} %cell_hbm.1, ...), custom_call_target="tpu_custom_call" | custom-call | tf_op jit(solution)/shard_map/prep/pallas_call | solution.py:359
  5.0 1.1 %collective-permute-done.hc = f32[8,8,128]{2,1,0:T(8,128)S(1)} collective-permute-done((f32[8,8,128]{2,1,0:T(8,128)S(1)}, f32[8,8,128]{2,1,0:T(8,128)S(1)}, u32[]{:S(2)}, u32[]{:S(2)}) %collective-permute-start) | collective-permute-done | bytes 32800 | tf_op jit(solution)/shard_map/ppermute | solution.py:354
  6.2 4.0 %collective-permute-start.1 = (f32[8,17,128]{2,1,0:T(8,128)S(1)}, f32[8,17,128]{2,1,0:T(8,128)S(1)}, u32[]{:S(2)}, u32[]{:S(2)}) collective-permute-start(f32[8,17,128]{2,1,0:T(8,128)S(1)} %pad_maximum_fusion), channel_id=1, source_target_pairs={{0,120},{1,121},{2,122},{3,123},{4,124},{5,125},{6,126},{7,127},{8... | collective-permute-start | bytes 208904 | tf_op jit(solution)/shard_map/ppermute | solution.py:354
  10.2 0.0 copy-done.1
  10.2 0.0 copy-done
  10.2 2.3 %early.1 = (f32[128,128]{1,0:T(8,128)S(1)}, f32[680,128]{1,0:T(8,128)S(1)}, f32[160,640]{1,0:T(8,128)S(1)}, f32[800,128]{1,0:T(8,128)S(1)}, f32[160,640]{1,0:T(8,128)S(1)}) custom-call(f32[512,128]{1,0:T(8,128)S(1)} %bitcast.8, f32[512,128]{1,0:T(8,128)S(1)} %bitcast.10, f32[8,8,128]{2,1,0:T(8,128)S(1)} %collective-permute-done.hc, ...), custom_call_target="tpu_custom_call" | custom-call | tf_op jit(solution)/shard_map/early/pallas_call | solution.py:359
  12.5 0.0 collective-permute-done.1.ha
  12.5 0.0 copy-start.4
  12.5 0.0 copy-start.5
  12.5 1.2 %late.1 = (f32[9,8,16,128]{3,2,1,0:T(8,128)S(1)}, f32[256,128]{1,0:T(8,128)S(1)}, f32[400,128]{1,0:T(8,128)S(1)}, f32[328,128]{1,0:T(8,128)S(1)}, f32[272,128]{1,0:T(8,128)S(1)}) custom-call(f32[8,17,128]{2,1,0:T(8,128)S(1)} %collective-permute-done.1.ha, f32[128,256]{1,0:T(8,128)S(1)} %get-tuple-element.42.stiff, ...), custom_call_target="tpu_custom_call" | custom-call | tf_op jit(solution)/shard_map/late/pallas_call | solution.py:359
  13.7 1.9 %collective-permute-start.2 = (f32[400,128]{1,0:T(8,128)S(1)}, f32[400,128]{1,0:T(8,128)S(1)}, u32[]{:S(2)}, u32[]{:S(2)}) collective-permute-start(f32[400,128]{1,0:T(8,128)S(1)} %get-tuple-element.55), channel_id=1, source_target_pairs={{0,8},{1,9},{2,10},{3,11},{4,12},{5,13},{6,14},{7,15},{8,16},{9,17... | collective-permute-start | bytes 614408 | tf_op jit(solution)/shard_map/ppermute | solution.py:354
  15.6 1.5 %collective-permute-start.3 = (f32[328,128]{1,0:T(8,128)S(1)}, f32[328,128]{1,0:T(8,128)S(1)}, u32[]{:S(2)}, u32[]{:S(2)}) collective-permute-start(f32[328,128]{1,0:T(8,128)S(1)} %get-tuple-element.56), channel_id=1, source_target_pairs={{0,1},{1,2},{2,3},{3,4},{4,5},{5,6},{6,7},{7,0},{8,9},{9,10},{10,1... | collective-permute-start | bytes 503816 | tf_op jit(solution)/shard_map/ppermute | solution.py:354
  17.1 1.3 %collective-permute-start.4 = (f32[272,128]{1,0:T(8,128)S(1)}, f32[272,128]{1,0:T(8,128)S(1)}, u32[]{:S(2)}, u32[]{:S(2)}) collective-permute-start(f32[272,128]{1,0:T(8,128)S(1)} %get-tuple-element.57), channel_id=1, source_target_pairs={{0,9},{1,10},{2,11},{3,12},{4,13},{5,14},{6,15},{8,17},{9,18},{10,... | collective-permute-start | bytes 417800 | tf_op jit(solution)/shard_map/ppermute | solution.py:354
  18.4 0.0 copy-start.2
  18.4 0.0 copy-start.3
  18.4 0.5 %own.1.part = f32[128,1024]{1,0:T(8,128)S(1)} custom-call(f32[256,128]{1,0:T(8,128)S(1)} %get-tuple-element.54.own), custom_call_target="tpu_custom_call" | custom-call | tf_op jit(solution)/shard_map/own/pallas_call | solution.py:359
  18.9 9.0 %collective-permute-done.4.got_sd = f32[272,128]{1,0:T(8,128)S(1)} collective-permute-done((f32[272,128]{1,0:T(8,128)S(1)}, f32[272,128]{1,0:T(8,128)S(1)}, u32[]{:S(2)}, u32[]{:S(2)}) %collective-permute-start.4) | collective-permute-done | bytes 139296 | tf_op jit(solution)/shard_map/ppermute | solution.py:354
  27.9 0.0 collective-permute-done.3.got_d
  27.9 0.0 collective-permute-done.2.got_s
  27.9 0.0 copy-done.4
  27.9 0.0 copy-done.5
  27.9 0.0 copy-done.2
  27.9 0.0 copy-done.3
  27.9 1.9 %final.1 = (f32[512,128]{1,0:T(8,128)}, f32[512,128]{1,0:T(8,128)}, f32[125,1024]{1,0:T(8,128)}) custom-call(f32[512,128]{1,0:T(8,128)S(1)} %bitcast.9, f32[512,128]{1,0:T(8,128)S(1)} %bitcast.12, f32[512,128]{1,0:T(8,128)S(1)} %bitcast.11, f32[512,128]{1,0:T(8,128)S(1)} %bitcast.13, f32[512,128]{1,0:T(8,128)S(1)} %bitcast.14, f32[512,128]{1,0:T(8,128)S(1)} %bitcast.15, ...), custom_call_target="tpu_custom_call" | custom-call | tf_op jit(solution)/shard_map/final/pallas_call | solution.py:359
  (2 shorter events, 0.0 us)
Async XLA Ops:
  0.6 1.7 %copy-start.6 = (s32[1,4]{1,0:T(1,128)S(1)}, s32[1,4]{1,0:T(1,128)}, u32[]{:S(2)}) copy-start(s32[1,4]{1,0:T(1,128)} %scount.1) | copy-start | bytes 52
  0.6 9.5 %copy-start.1 = (f32[4,8,16,128]{3,2,1,0:T(8,128)S(1)}, f32[4,8,16,128]{3,2,1,0:T(8,128)}, u32[]{:S(2)}) copy-start(f32[4,8,16,128]{3,2,1,0:T(8,128)} %adj.1) | copy-start | bytes 786436
  1.6 8.6 %copy-start = (f32[4,8,16,128]{3,2,1,0:T(8,128)S(1)}, f32[4,8,16,128]{3,2,1,0:T(8,128)}, u32[]{:S(2)}) copy-start(f32[4,8,16,128]{3,2,1,0:T(8,128)} %wave.1) | copy-start | bytes 786436
  1.6 4.6 %collective-permute-start = (f32[8,8,128]{2,1,0:T(8,128)S(1)}, f32[8,8,128]{2,1,0:T(8,128)S(1)}, u32[]{:S(2)}, u32[]{:S(2)}) collective-permute-start(f32[8,8,128]{2,1,0:T(8,128)S(1)} %get-tuple-element.32), channel_id=1, source_target_pairs={{0,7},{1,0},{2,1},{3,2},{4,3},{5,4},{6,5},{7,6},{8,15},{9,8},{10,9... | collective-permute-start | bytes 98312 | tf_op jit(solution)/shard_map/ppermute | solution.py:354
  6.2 6.3 %collective-permute-start.1 = (f32[8,17,128]{2,1,0:T(8,128)S(1)}, f32[8,17,128]{2,1,0:T(8,128)S(1)}, u32[]{:S(2)}, u32[]{:S(2)}) collective-permute-start(f32[8,17,128]{2,1,0:T(8,128)S(1)} %pad_maximum_fusion), channel_id=1, source_target_pairs={{0,120},{1,121},{2,122},{3,123},{4,124},{5,125},{6,126},{7,127},{8... | collective-permute-start | bytes 208904 | tf_op jit(solution)/shard_map/ppermute | solution.py:354
  12.5 15.4 %copy-start.4 = (f32[4,8,16,128]{3,2,1,0:T(8,128)S(1)}, f32[4,8,16,128]{3,2,1,0:T(8,128)}, u32[]{:S(2)}) copy-start(f32[4,8,16,128]{3,2,1,0:T(8,128)} %param.16) | copy-start | bytes 786436
  12.5 15.4 %copy-start.5 = (f32[4,8,16,128]{3,2,1,0:T(8,128)S(1)}, f32[4,8,16,128]{3,2,1,0:T(8,128)}, u32[]{:S(2)}) copy-start(f32[4,8,16,128]{3,2,1,0:T(8,128)} %param.17) | copy-start | bytes 786436
  13.7 14.2 %collective-permute-start.2 = (f32[400,128]{1,0:T(8,128)S(1)}, f32[400,128]{1,0:T(8,128)S(1)}, u32[]{:S(2)}, u32[]{:S(2)}) collective-permute-start(f32[400,128]{1,0:T(8,128)S(1)} %get-tuple-element.55), channel_id=1, source_target_pairs={{0,8},{1,9},{2,10},{3,11},{4,12},{5,13},{6,14},{7,15},{8,16},{9,17... | collective-permute-start | bytes 614408 | tf_op jit(solution)/shard_map/ppermute | solution.py:354
  15.6 12.2 %collective-permute-start.3 = (f32[328,128]{1,0:T(8,128)S(1)}, f32[328,128]{1,0:T(8,128)S(1)}, u32[]{:S(2)}, u32[]{:S(2)}) collective-permute-start(f32[328,128]{1,0:T(8,128)S(1)} %get-tuple-element.56), channel_id=1, source_target_pairs={{0,1},{1,2},{2,3},{3,4},{4,5},{5,6},{6,7},{7,0},{8,9},{9,10},{10,1... | collective-permute-start | bytes 503816 | tf_op jit(solution)/shard_map/ppermute | solution.py:354
  17.1 10.8 %collective-permute-start.4 = (f32[272,128]{1,0:T(8,128)S(1)}, f32[272,128]{1,0:T(8,128)S(1)}, u32[]{:S(2)}, u32[]{:S(2)}) collective-permute-start(f32[272,128]{1,0:T(8,128)S(1)} %get-tuple-element.57), channel_id=1, source_target_pairs={{0,9},{1,10},{2,11},{3,12},{4,13},{5,14},{6,15},{8,17},{9,18},{10,... | collective-permute-start | bytes 417800 | tf_op jit(solution)/shard_map/ppermute | solution.py:354
  18.4 9.5 %copy-start.2 = (f32[4,8,16,128]{3,2,1,0:T(8,128)S(1)}, f32[4,8,16,128]{3,2,1,0:T(8,128)}, u32[]{:S(2)}) copy-start(f32[4,8,16,128]{3,2,1,0:T(8,128)} %param.13) | copy-start | bytes 786436
  18.4 9.5 %copy-start.3 = (f32[4,8,16,128]{3,2,1,0:T(8,128)S(1)}, f32[4,8,16,128]{3,2,1,0:T(8,128)}, u32[]{:S(2)}) copy-start(f32[4,8,16,128]{3,2,1,0:T(8,128)} %param.15) | copy-start | bytes 786436

commit v2 on v1

--- a/solution.py
+++ b/solution.py
@@ -12,6 +12,7 @@
 BF16 = jnp.bfloat16
 DT = 0.05
 NT = (((1,), (1,)), ((), ()))
+CHUNKS = 2
 NROW = 85
 PLANE = 128
 
@@ -236,13 +237,13 @@
 
 def late_kernel(
     ha, stiff, spread, fold, wcol, kern_low, ng_low, mass, targ, val_up, prod_up, frc_up,
-    inner, own, buf_s, buf_d, buf_sd, kern, ng, g, lhs, val, prod, frc,
+    ng, own, buf_s, buf_d, buf_sd, kern, g, lhs, val, prod, frc,
 ):
     keep_d = (lax.axis_index("depth") < lax.axis_size("depth") - 1).astype(F32)
     keep_s = (lax.axis_index("surf") < lax.axis_size("surf") - 1).astype(F32)
     for x in range(8):
-        g[x * 17 : x * 17 + 16, :] = ha[x, 0:16, :] * keep_s
-        g[x * 17 + 16 : x * 17 + 17, :] = ha[x, 16:17, :] * (keep_s * keep_d)
+        g[x * 17 : x * 17 + 16, :] = ha[x * 16 : x * 16 + 16, :] * keep_s
+        g[x * 17 + 16 : x * 17 + 17, :] = ha[128 + x : 129 + x, :] * (keep_s * keep_d)
     load_plane(g, 17, 0, lhs, 0)
     val[...] = dot2(lhs[0:40, :], spread[...])
     inside_plane(1, 4, val, 0, stiff, prod, frc)
@@ -256,47 +257,54 @@
     for x in range(8):
         base = x * NROW
         for a in range(8):
+            at = base + a * 17 + 16
             if a < 4:
-                rows = ng_low[base + a * 17 : base + a * 17 + 17, :]
+                row = ng_low[at : at + 1, :]
             elif a == 4:
-                rows = ng_low[base + 68 : base + 85, :] + ng[base : base + 17, :]
+                row = ng_low[at : at + 1, :] + ng[base + 16 : base + 17, :]
             else:
-                at = base + (a - 4) * 17
-                rows = ng[at : at + 17, :]
-            inner[x, a] = rows[0:16]
-            buf_d[256 + x * 8 + a : 257 + x * 8 + a, :] = rows[16:17]
+                row = ng[at - 68 : at - 67, :]
+            buf_d[256 + x * 8 + a : 257 + x * 8 + a, :] = row
         buf_s[256 + x * 16 : 272 + x * 16, :] = ng[base + 68 : base + 84, :]
         buf_sd[256 + x : 257 + x, :] = ng[base + 84 : base + 85, :]
     for a in range(8):
-        inner[8, a] = mass[a * 17 : a * 17 + 16, :]
         buf_d[320 + a : 321 + a, :] = mass[a * 17 + 16 : a * 17 + 17, :]
     buf_s[384:400, :] = mass[136:152, :]
     buf_sd[264:265, :] = mass[152:153, :]
     buf_sd[265:272, :] = jnp.zeros((7, 128), F32)
 
 
-def add_bricks(acc, buf, rows):
+def add_bricks(acc, buf, first=0, count=1024):
+    bricks = lax.broadcasted_iota(jnp.int32, (count, 128), 0).astype(F32) + float(first)
     for ea in range(2):
         block = buf[ea * 128 : ea * 128 + 128, :]
-        hit = jnp.where(rows == block[125:126, :], 1.0, 0.0).astype(BF16)
+        hit = jnp.where(bricks == block[125:126, :], 1.0, 0.0).astype(BF16)
         term = dot2(block, hit, NT)
         acc = term if acc is None else acc + term
     return acc
 
 
-def own_kernel(own, part):
-    rows = lax.broadcasted_iota(jnp.int32, (1024, 128), 0).astype(F32)
-    part[...] = add_bricks(None, own, rows)
+def near_kernel(own, got_d, ng_low, ng, mass, near, inner):
+    near[...] = add_bricks(add_bricks(None, own), got_d)
+    for x in range(8):
+        for a in range(8):
+            low, high = x * NROW + a * 17, x * NROW + (a - 4) * 17
+            if a < 4:
+                inner[x, a] = ng_low[low : low + 16, :]
+            elif a == 4:
+                inner[x, a] = ng_low[low : low + 16, :] + ng[high : high + 16, :]
+            else:
+                inner[x, a] = ng[high : high + 16, :]
+    for a in range(8):
+        inner[8, a] = mass[a * 17 : a * 17 + 16, :]
 
 
 def final_kernel(
-    wave, wave_old, adj, adj_old, src, adj_src, inner, part, got_s, got_d, got_sd,
+    wave, wave_old, adj, adj_old, src, adj_src, inner, near, got_s, got_d, got_sd,
     wave_next, adj_next, bricks, wave_buf, adj_buf, brick_buf, sem,
 ):
-    has_s = lax.axis_index("surf") > 0
-    has_d = lax.axis_index("depth") > 0
-    keep_s = has_s.astype(F32)
-    keep_d = has_d.astype(F32)
+    keep_s = (lax.axis_index("surf") > 0).astype(F32)
+    keep_d = (lax.axis_index("depth") > 0).astype(F32)
     first = lax.broadcasted_iota(jnp.int32, (16, 128), 0) == 0
 
     def total(ch, a):
@@ -321,12 +329,11 @@
     ]
     for c in copies:
         c.start()
-    for k in range(2):
-        cols = slice(k * 512, k * 512 + 512)
-        rows = lax.broadcasted_iota(jnp.int32, (512, 128), 0).astype(F32) + float(k * 512)
-        acc = part[:, cols]
-        for buf in (got_s, got_d, got_sd):
-            acc = add_bricks(acc, buf, rows)
+    for k in range(CHUNKS):
+        cols = slice(k * (1024 // CHUNKS), (k + 1) * (1024 // CHUNKS))
+        acc = near[:, cols]
+        for buf in (got_s, got_sd):
+            acc = add_bricks(acc, buf, k * (1024 // CHUNKS), 1024 // CHUNKS)
         brick_buf[:, cols] = acc[0:125, :]
         copy = pltpu.make_async_copy(brick_buf.at[:, cols], bricks.at[:, cols], sem.at[2 + k])
         copy.start()
@@ -400,7 +407,7 @@
     )
     hc, plane, prep = lax.optimization_barrier((hc, plane, tuple(prep)))
     stiff, mass, targ, spread, fold, wcol = prep
-    ha = send(jnp.concatenate([plane, hc[:, 0:1]], 1), -1, 0, True, True)
+    ha = send(jnp.concatenate([plane.reshape(128, 128), hc[:, 0]], 0), -1, 0, True, True)
 
     kern_low, ng_low, val_up, prod_up, frc_up = call(
         early_kernel,
@@ -409,24 +416,26 @@
         (out(128, 128), out(8 * NROW, 128), out(160, 640), out(800, 128), out(160, 640)),
         [vmem(8 * NROW, 128), vmem(200, 512), vmem(200, 640), vmem(1000, 128), vmem(200, 640)],
     )
-    inner, own, buf_s, buf_d, buf_sd = call(
+    ng, own, buf_s, buf_d, buf_sd = call(
         late_kernel,
         "late",
         (ha, stiff, spread, fold, wcol, kern_low, ng_low, mass, targ, val_up, prod_up, frc_up),
-        (out(9, 8, 16, 128), out(256, 128), out(400, 128), out(328, 128), out(272, 128)),
-        [vmem(128, 128), vmem(8 * NROW, 128), vmem(8 * 17, 128), vmem(200, 512), vmem(40, 640),
+        (out(8 * NROW, 128), out(256, 128), out(400, 128), out(328, 128), out(272, 128)),
+        [vmem(128, 128), vmem(8 * 17, 128), vmem(200, 512), vmem(40, 640),
          vmem(1000, 128), vmem(200, 640)],
     )
-    got_s = send(buf_s, 1, 0, False, True)
+    got_s = send(buf_s, 1, 0, True, True)
     got_d = send(buf_d, 0, 1, True, True)
     got_sd = send(buf_sd, 1, 1, False, False)
-    (part,) = call(own_kernel, "own", (own,), (out(128, 1024),))
+    near, inner = call(
+        near_kernel, "near", (own, got_d, ng_low, ng, mass), (out(128, 1024), out(9, 8, 16, 128))
+    )
     wave_next, adj_next, bricks = call(
         final_kernel,
         "final",
-        (wave, wave_old, adj, adj_old, source, adj_source, inner, part, got_s, got_d, got_sd),
+        (wave, wave_old, adj, adj_old, source, adj_source, inner, near, got_s, got_d, got_sd),
         (out(4 * PLANE, 128), out(4 * PLANE, 128), out(125, 1024)),
-        [vmem(4 * PLANE, 128), vmem(4 * PLANE, 128), vmem(125, 1024), pltpu.SemaphoreType.DMA((4,))],
+        [vmem(4 * PLANE, 128), vmem(4 * PLANE, 128), vmem(125, 1024), pltpu.SemaphoreType.DMA((2 + CHUNKS,))],
         out_space=pl.ANY,
     )
     return wave_next.reshape(shape), adj_next.reshape(shape), bricks

time: 30 us -> 28 us (0.933)
  the two profiles are of different devices: /device:TPU:31 before, /device:TPU:7 now
where the time goes in v2:
time: 28 us; the launch traced here: 27.8 us
  Pallas kernels  9.46 us (34%)
  starting transfers between devices  9.16 us (33%)
  waiting for transfers between devices  8.33 us (30%)
  between operations  0.76 us (3%)
    pallas_call x6, Pallas kernels, call(): pl.pallas_call(kernel, out_shape=tuple(outs), in_specs=specs or [here] *...  9.46 us
    ppermute x5, starting transfers between devices, send(): return lax.ppermute(x, ('surf', 'depth'), pairs)  9.16 us
    ppermute x5, waiting for transfers between devices, send(): return lax.ppermute(x, ('surf', 'depth'), pairs)  8.33 us
  transfers between devices with their start and end apart: 5, of which 3 were waited for; matrix products, arithmetic and copies ran while one was open for 0% of the time, Pallas kernels for 21%

profile of v2, /device:TPU:7, one launch (start us, length us, event | category | flops | bytes accessed | tf_op | source)
XLA Modules:
  0.0 27.8 jit_solution(10582419141423238352)
XLA Ops:
  0.6 0.0 copy-start.6
  0.6 0.9 %pack.1 = (f32[8,8,128]{2,1,0:T(8,128)S(1)}, f32[8,16,128]{2,1,0:T(8,128)S(1)}) custom-call(f32[4,8,16,128]{3,2,1,0:T(8,128)} %wave.1, f32[4,8,16,128]{3,2,1,0:T(8,128)} %adj.1), custom_call_target="tpu_custom_call" | custom-call | tf_op jit(solution)/shard_map/pack/pallas_call | solution.py:366
  1.5 0.0 copy-start.1
  1.6 0.0 copy-start
  1.6 0.7 %collective-permute-start = (f32[8,8,128]{2,0,1:T(8,128)S(1)}, f32[8,8,128]{2,0,1:T(8,128)S(1)}, u32[]{:S(2)}, u32[]{:S(2)}) collective-permute-start(f32[8,8,128]{2,0,1:T(8,128)S(1)} %copy.15), channel_id=1, source_target_pairs={{0,7},{1,0},{2,1},{3,2},{4,3},{5,4},{6,5},{7,6},{8,15},{9,8},{10,9... | collective-permute-start | bytes 98312 | tf_op jit(solution)/shard_map/ppermute | solution.py:361
  2.2 0.0 copy-done.6
  2.3 2.7 %prep.1 = (f32[128,256]{1,0:T(8,128)S(1)}, f32[160,128]{1,0:T(8,128)S(1)}, f32[8,256]{1,0:T(8,128)S(1)}, bf16[512,640]{1,0:T(8,128)(2,1)S(1)}, bf16[640,512]{1,0:T(8,128)(2,1)S(1)}, /*index=5*/f32[128,128]{1,0:T(8,128)S(1)}) custom-call(f32[125,256]{1,0:T(8,128)} %dens_hbm.1, f32[125,256]{1,0:T(8,128)} %modu_hbm.1, s32[1,256]{1,0:T(1,128)} %cell_hbm.1, ...), custom_call_target="tpu_custom_call" | custom-call | tf_op jit(solution)/shard_map/prep/pallas_call | solution.py:366
  5.0 1.1 %collective-permute-done = f32[8,8,128]{2,0,1:T(8,128)S(1)} collective-permute-done((f32[8,8,128]{2,0,1:T(8,128)S(1)}, f32[8,8,128]{2,0,1:T(8,128)S(1)}, u32[]{:S(2)}, u32[]{:S(2)}) %collective-permute-start) | collective-permute-done | bytes 32800 | tf_op jit(solution)/shard_map/ppermute | solution.py:361
  6.1 6.3 %collective-permute-start.1 = (f32[136,128]{1,0:T(8,128)S(1)}, f32[136,128]{1,0:T(8,128)S(1)}, u32[]{:S(2)}, u32[]{:S(2)}) collective-permute-start(f32[136,128]{1,0:T(8,128)S(1)} %pad_maximum_fusion), channel_id=1, source_target_pairs={{0,120},{1,121},{2,122},{3,123},{4,124},{5,125},{6,126},{7,127},{8... | collective-permute-start | bytes 208904 | tf_op jit(solution)/shard_map/ppermute | solution.py:361
  12.4 0.0 copy-done.1
  12.4 0.0 copy-done
  12.4 2.3 %early.1 = (f32[128,128]{1,0:T(8,128)S(1)}, f32[680,128]{1,0:T(8,128)S(1)}, f32[160,640]{1,0:T(8,128)S(1)}, f32[800,128]{1,0:T(8,128)S(1)}, f32[160,640]{1,0:T(8,128)S(1)}) custom-call(f32[512,128]{1,0:T(8,128)S(1)} %bitcast.11, f32[512,128]{1,0:T(8,128)S(1)} %bitcast.13, f32[8,8,128]{2,1,0:T(8,128)S(1)} %copy.16.hc, ...), custom_call_target="tpu_custom_call" | custom-call | tf_op jit(solution)/shard_map/early/pallas_call | solution.py:366
  14.7 0.0 collective-permute-done.1.ha
  14.7 1.2 %late.1 = (f32[680,128]{1,0:T(8,128)S(1)}, f32[256,128]{1,0:T(8,128)S(1)}, f32[400,128]{1,0:T(8,128)S(1)}, f32[328,128]{1,0:T(8,128)S(1)}, f32[272,128]{1,0:T(8,128)S(1)}) custom-call(f32[136,128]{1,0:T(8,128)S(1)} %collective-permute-done.1.ha, f32[128,256]{1,0:T(8,128)S(1)} %get-tuple-element.44.stiff, bf16[512,640]{1,0:T(8,128)(2,1)S(1)} %get-tuple-element.45.spread, ...), custom_call_target="tpu_custom_call" | custom-call | tf_op jit(solution)/shard_map/late/pallas_call | solution.py:366
  15.9 0.1 collective-permute-start.3
  16.0 1.5 %collective-permute-start.2 = (f32[328,128]{1,0:T(8,128)S(1)}, f32[328,128]{1,0:T(8,128)S(1)}, u32[]{:S(2)}, u32[]{:S(2)}) collective-permute-start(f32[328,128]{1,0:T(8,128)S(1)} %get-tuple-element.56), channel_id=1, source_target_pairs={{0,1},{1,2},{2,3},{3,4},{4,5},{5,6},{6,7},{7,0},{8,9},{9,10},{10,1... | collective-permute-start | bytes 503816 | tf_op jit(solution)/shard_map/ppermute | solution.py:361
  17.5 0.7 %collective-permute-start.4 = (f32[272,128]{1,0:T(8,128)S(1)}, f32[272,128]{1,0:T(8,128)S(1)}, u32[]{:S(2)}, u32[]{:S(2)}) collective-permute-start(f32[272,128]{1,0:T(8,128)S(1)} %get-tuple-element.61), channel_id=1, source_target_pairs={{0,9},{1,10},{2,11},{3,12},{4,13},{5,14},{6,15},{8,17},{9,18},{10,... | collective-permute-start | bytes 417800 | tf_op jit(solution)/shard_map/ppermute | solution.py:361
  18.1 1.6 %collective-permute-done.2.got_d = f32[328,128]{1,0:T(8,128)S(1)} collective-permute-done((f32[328,128]{1,0:T(8,128)S(1)}, f32[328,128]{1,0:T(8,128)S(1)}, u32[]{:S(2)}, u32[]{:S(2)}) %collective-permute-start.2) | collective-permute-done | bytes 167968 | tf_op jit(solution)/shard_map/ppermute | solution.py:361
  19.8 0.0 copy-start.2
  19.8 0.0 copy-start.3
  19.8 0.0 copy-start.4
  19.8 0.0 copy-start.5
  19.8 0.7 %near.1 = (f32[128,1024]{1,0:T(8,128)S(1)}, f32[9,8,16,128]{3,2,1,0:T(8,128)S(1)}) custom-call(f32[256,128]{1,0:T(8,128)S(1)} %get-tuple-element.55.own, f32[328,128]{1,0:T(8,128)S(1)} %collective-permute-done.2.got_d, f32[680,128]{1,0:T(8,128)S(1)} %get-tuple-element.49.ng_low, f32[680,128]{1,0:T(8,128)S(1)} %get-tuple-element.57.ng, ...), custom_call_target="tpu_custom_call" | custom-call | tf_op jit(solution)/shard_map/near/pallas_call | solution.py:366
  20.5 0.0 collective-permute-done.4.got_sd
  20.5 5.6 %collective-permute-done.3.got_s = f32[400,128]{1,0:T(8,128)S(1)} collective-permute-done((f32[400,128]{1,0:T(8,128)S(1)}, f32[400,128]{1,0:T(8,128)S(1)}, u32[]{:S(2)}, u32[]{:S(2)}) %collective-permute-start.3) | collective-permute-done | bytes 204832 | tf_op jit(solution)/shard_map/ppermute | solution.py:361
  26.1 0.0 copy-done.2
  26.1 0.0 copy-done.3
  26.1 0.0 copy-done.4
  26.1 0.0 copy-done.5
  26.1 1.7 %final.1 = (f32[512,128]{1,0:T(8,128)}, f32[512,128]{1,0:T(8,128)}, f32[125,1024]{1,0:T(8,128)}) custom-call(f32[512,128]{1,0:T(8,128)S(1)} %bitcast.12, f32[512,128]{1,0:T(8,128)S(1)} %bitcast.15, f32[512,128]{1,0:T(8,128)S(1)} %bitcast.14, f32[512,128]{1,0:T(8,128)S(1)} %bitcast.16, f32[512,128]{1,0:T(8,128)S(1)} %bitcast.17, f32[512,128]{1,0:T(8,128)S(1)} %bitcast.18, ...), custom_call_target="tpu_custom_call" | custom-call | tf_op jit(solution)/shard_map/final/pallas_call | solution.py:366
  (4 shorter events, 0.0 us)
Async XLA Ops:
  0.6 1.6 %copy-start.6 = (s32[1,4]{1,0:T(1,128)S(1)}, s32[1,4]{1,0:T(1,128)}, u32[]{:S(2)}) copy-start(s32[1,4]{1,0:T(1,128)} %scount.1) | copy-start | bytes 52
  1.5 10.9 %copy-start.1 = (f32[4,8,16,128]{3,2,1,0:T(8,128)S(1)}, f32[4,8,16,128]{3,2,1,0:T(8,128)}, u32[]{:S(2)}) copy-start(f32[4,8,16,128]{3,2,1,0:T(8,128)} %adj.1) | copy-start | bytes 786436
  1.6 10.9 %copy-start = (f32[4,8,16,128]{3,2,1,0:T(8,128)S(1)}, f32[4,8,16,128]{3,2,1,0:T(8,128)}, u32[]{:S(2)}) copy-start(f32[4,8,16,128]{3,2,1,0:T(8,128)} %wave.1) | copy-start | bytes 786436
  1.6 4.6 %collective-permute-start = (f32[8,8,128]{2,0,1:T(8,128)S(1)}, f32[8,8,128]{2,0,1:T(8,128)S(1)}, u32[]{:S(2)}, u32[]{:S(2)}) collective-permute-start(f32[8,8,128]{2,0,1:T(8,128)S(1)} %copy.15), channel_id=1, source_target_pairs={{0,7},{1,0},{2,1},{3,2},{4,3},{5,4},{6,5},{7,6},{8,15},{9,8},{10,9... | collective-permute-start | bytes 98312 | tf_op jit(solution)/shard_map/ppermute | solution.py:361
  6.1 8.6 %collective-permute-start.1 = (f32[136,128]{1,0:T(8,128)S(1)}, f32[136,128]{1,0:T(8,128)S(1)}, u32[]{:S(2)}, u32[]{:S(2)}) collective-permute-start(f32[136,128]{1,0:T(8,128)S(1)} %pad_maximum_fusion), channel_id=1, source_target_pairs={{0,120},{1,121},{2,122},{3,123},{4,124},{5,125},{6,126},{7,127},{8... | collective-permute-start | bytes 208904 | tf_op jit(solution)/shard_map/ppermute | solution.py:361
  15.9 10.2 %collective-permute-start.3 = (f32[400,128]{1,0:T(8,128)S(1)}, f32[400,128]{1,0:T(8,128)S(1)}, u32[]{:S(2)}, u32[]{:S(2)}) collective-permute-start(f32[400,128]{1,0:T(8,128)S(1)} %get-tuple-element.60), channel_id=1, source_target_pairs={{0,8},{1,9},{2,10},{3,11},{4,12},{5,13},{6,14},{7,15},{8,16},{9,17... | collective-permute-start | bytes 614408 | tf_op jit(solution)/shard_map/ppermute | solution.py:361
  16.0 3.8 %collective-permute-start.2 = (f32[328,128]{1,0:T(8,128)S(1)}, f32[328,128]{1,0:T(8,128)S(1)}, u32[]{:S(2)}, u32[]{:S(2)}) collective-permute-start(f32[328,128]{1,0:T(8,128)S(1)} %get-tuple-element.56), channel_id=1, source_target_pairs={{0,1},{1,2},{2,3},{3,4},{4,5},{5,6},{6,7},{7,0},{8,9},{9,10},{10,1... | collective-permute-start | bytes 503816 | tf_op jit(solution)/shard_map/ppermute | solution.py:361
  17.5 3.1 %collective-permute-start.4 = (f32[272,128]{1,0:T(8,128)S(1)}, f32[272,128]{1,0:T(8,128)S(1)}, u32[]{:S(2)}, u32[]{:S(2)}) collective-permute-start(f32[272,128]{1,0:T(8,128)S(1)} %get-tuple-element.61), channel_id=1, source_target_pairs={{0,9},{1,10},{2,11},{3,12},{4,13},{5,14},{6,15},{8,17},{9,18},{10,... | collective-permute-start | bytes 417800 | tf_op jit(solution)/shard_map/ppermute | solution.py:361
  19.8 6.3 %copy-start.2 = (f32[4,8,16,128]{3,2,1,0:T(8,128)S(1)}, f32[4,8,16,128]{3,2,1,0:T(8,128)}, u32[]{:S(2)}) copy-start(f32[4,8,16,128]{3,2,1,0:T(8,128)} %param.13) | copy-start | bytes 786436
  19.8 6.3 %copy-start.3 = (f32[4,8,16,128]{3,2,1,0:T(8,128)S(1)}, f32[4,8,16,128]{3,2,1,0:T(8,128)}, u32[]{:S(2)}) copy-start(f32[4,8,16,128]{3,2,1,0:T(8,128)} %param.15) | copy-start | bytes 786436
  19.8 6.3 %copy-start.4 = (f32[4,8,16,128]{3,2,1,0:T(8,128)S(1)}, f32[4,8,16,128]{3,2,1,0:T(8,128)}, u32[]{:S(2)}) copy-start(f32[4,8,16,128]{3,2,1,0:T(8,128)} %param.16) | copy-start | bytes 786436
  19.8 6.3 %copy-start.5 = (f32[4,8,16,128]{3,2,1,0:T(8,128)S(1)}, f32[4,8,16,128]{3,2,1,0:T(8,128)}, u32[]{:S(2)}) copy-start(f32[4,8,16,128]{3,2,1,0:T(8,128)} %param.17) | copy-start | bytes 786436

commit v3 on v2

--- a/solution.py
+++ b/solution.py
@@ -14,6 +14,7 @@
 NT = (((1,), (1,)), ((), ()))
 CHUNKS = 2
 NROW = 85
+COLUMN = 136
 PLANE = 128
 
 
@@ -49,6 +50,11 @@
 
 def dot2(x, table, dims=(((1,), (0,)), ((), ()))):
     hi, lo = split2(x)
+    rows = x.shape[0]
+    if rows % 16 == 0:
+        both = jnp.concatenate([hi, lo], axis=0)
+        both = lax.dot_general(both, table, dims, preferred_element_type=F32)
+        return both[0:rows] + both[rows:]
     return lax.dot_general(hi, table, dims, preferred_element_type=F32) + lax.dot_general(
         lo, table, dims, preferred_element_type=F32
     )
@@ -67,19 +73,25 @@
 
 
 def prep_kernel(
-    dens_hbm, modu_hbm, cell_hbm, selem_hbm, sbrick_hbm, scount, stiff, mass, targ, spread, fold, wcol,
-    dens, modu, cell, selem, sbrick, sem, ms0, ms1, mo,
+    wave_hbm, adj_hbm, dens_hbm, modu_hbm, cell_hbm, selem_hbm, sbrick_hbm, scount_hbm,
+    fields, stiff, mass, targ, spread, fold, wcol,
+    dens, modu, cell, selem, sbrick, scount, sem, ms0, ms1, mo,
 ):
     pairs = (
-        (dens_hbm, dens), (modu_hbm, modu), (cell_hbm, cell), (selem_hbm, selem), (sbrick_hbm, sbrick)
+        (dens_hbm, dens), (modu_hbm, modu), (cell_hbm, cell), (selem_hbm, selem), (sbrick_hbm, sbrick),
+        (scount_hbm, scount),
     )
     copies = [pltpu.make_async_copy(a, b, sem.at[k]) for k, (a, b) in enumerate(pairs)]
-    for c in copies:
+    late_copies = []
+    for x in range(8):
+        src = (wave_hbm if x < 4 else adj_hbm).at[pl.ds(x % 4 * PLANE, PLANE)]
+        late_copies.append(pltpu.make_async_copy(src, fields.at[pl.ds(x * COLUMN, PLANE)], sem.at[6 + x]))
+    for c in copies + late_copies:
         c.start()
     sub = lax.broadcasted_iota(jnp.int32, (128, 128), 0)
     lane = lax.broadcasted_iota(jnp.int32, (128, 128), 1)
     fold[...] = jnp.zeros(fold.shape, BF16)
-    for r in range(5):
+    for r in range(4):
         node = (4 * (lane & 31) + r) & 127
         hit = sub == node
         for ec in range(4):
@@ -109,14 +121,20 @@
     stiff[0:125, :] = dot2(dens[...], place, NT) * both
     cells = dot2(modu[...], place, NT) * both
     mass[...] = jnp.zeros(mass.shape, F32)
+    lined = []
     for ea, ms in ((0, ms0), (1, ms1)):
         ms[0:125, :] = cells[:, ea * 128 : ea * 128 + 128]
-        rows = jnp.concatenate([ms[pl.ds(r, 25, stride=5), :] for r in range(5)], axis=1)
-        mo[...] = dot2(rows, fold[...])
+        ms[125:160, :] = jnp.zeros((35, 128), F32)
+        parts = [ms[pl.ds(r, 32, stride=5), :] for r in range(5)]
+        parts[0] = parts[0] + to_next(parts.pop())
+        lined.append(jnp.concatenate(parts, axis=1))
+    mo[...] = dot2(jnp.concatenate(lined, axis=0), fold[...])
+    for ea in range(2):
         for p in range(5):
             for ec in range(4):
                 at = pl.ds((4 * ea + p) * 17 + 4 * ec, 5)
-                mass[at, :] = mass[at, :] + mo[p * 5 : p * 5 + 5, ec * 128 : ec * 128 + 128]
+                row = ea * 32 + p * 5
+                mass[at, :] = mass[at, :] + mo[row : row + 5, ec * 128 : ec * 128 + 128]
     sub = lax.broadcasted_iota(jnp.int32, (8, 256), 0)
     lane = lax.broadcasted_iota(jnp.int32, (1, 256), 1)
     elem_iota = lax.broadcasted_iota(jnp.int32, (256, 256), 0)
@@ -132,16 +150,34 @@
         )
     at_cell = lax.dot_general(acc.astype(BF16), place, NT, preferred_element_type=F32)
     targ[0:4, :] = 32.0 * at_cell[0:4] + at_cell[4:8] - 1.0
-
-
-def load_plane(g, step, p, lhs, row):
+    for c in late_copies:
+        c.wait()
+
+
+def load_plane(row_of, lhs, row):
     for c in range(17):
-        tile = g[pl.ds(p * 17 + c, 8, stride=step), :]
+        tile = row_of(c)
         if c < 16:
             at = row + c % 4 * 8
             lhs[at : at + 8, c // 4 * 128 : c // 4 * 128 + 128] = tile
         if c % 4 == 0 and c > 0:
             lhs[row + 32 : row + 40, (c // 4 - 1) * 128 : c // 4 * 128] = tile
+
+
+def from_next(x):
+    last = (lax.broadcasted_iota(jnp.int32, x.shape, 1) & 31) == 31
+    return jnp.where(last, pltpu.roll(x, 31, 1), pltpu.roll(x, 127, 1))
+
+
+def to_next(x):
+    zeroth = (lax.broadcasted_iota(jnp.int32, x.shape, 1) & 31) == 0
+    return jnp.where(zeroth, pltpu.roll(x, 97, 1), pltpu.roll(x, 1, 1))
+
+
+def spread_planes(val, row, planes, spread):
+    nodes = dot2(planes, spread[...])
+    val[row : row + planes.shape[0], 0:512] = nodes
+    val[row : row + planes.shape[0], 512:640] = from_next(nodes[:, 0:128])
 
 
 def node_tile(p, q, r):
@@ -196,7 +232,8 @@
         total = sum(prod[pl.ds(j * 64 + t, count, stride=8), :] for t in range(4))
         kern[j * 8 : j * 8 + count, :] = total * wcol[j * 8 : j * 8 + count, :]
     kern[125:128, :] = jnp.zeros((3, 128), F32)
-    lhs[...] = dot2(frc[...], fold[...])
+    zeroth = frc[:, 0:128] + to_next(frc[:, 512:640])
+    lhs[...] = dot2(jnp.concatenate([zeroth, frc[:, 128:512]], axis=1), fold[...])
     for p in range(5):
         for c in range(17):
             parts = []
@@ -210,42 +247,47 @@
 
 
 def early_kernel(
-    wave, adj, hc, stiff, spread, fold, wcol, kern, ng, val_up, prod_up, frc_up, g, lhs, val, prod, frc
+    fields, hc, stiff, spread, fold, wcol, kern, ng, val_up, prod_up, frc_up, lhs, val, prod, frc
 ):
     keep = (lax.axis_index("depth") < lax.axis_size("depth") - 1).astype(F32)
-    for ea, planes in ((0, 5), (1, 4)):
-        for x in range(8):
-            src = wave if x < 4 else adj
-            for p in range(planes):
-                at = x * NROW + p * 17
-                row = x % 4 * PLANE + (4 * ea + p) * 16
-                g[at : at + 16, :] = src[row : row + 16, :]
-                g[at + 16 : at + 17, :] = hc[x, 4 * ea + p : 4 * ea + p + 1, :] * keep
-        for p in range(planes):
-            load_plane(g, NROW, p, lhs, p * 40)
-        if ea == 0:
-            val[...] = dot2(lhs[...], spread[...])
-            for p in range(5):
-                inside_plane(0, p, val, p, stiff, prod, frc)
-            across_planes(0, val, lambda q, r: val[node_tile(4, q, r)], stiff, prod, frc, prod, frc)
-            finish_layer(prod, frc, lhs, fold, wcol, kern, ng)
-        else:
-            val_up[...] = dot2(lhs[0:160, :], spread[...])
-            for p in range(4):
-                inside_plane(1, p, val_up, p, stiff, prod_up, frc_up)
+
+    def field_row(a):
+        def row_of(c):
+            if c == 16:
+                return hc[pl.ds(a, 8, stride=8), :] * keep
+            return fields[pl.ds(a * 16 + c, 8, stride=COLUMN), :]
+
+        return row_of
+
+    for a in range(5):
+        load_plane(field_row(a), lhs, a * 40)
+    spread_planes(val, 0, lhs[...], spread)
+    for p in range(5):
+        inside_plane(0, p, val, p, stiff, prod, frc)
+    across_planes(0, val, lambda q, r: val[node_tile(4, q, r)], stiff, prod, frc, prod, frc)
+    finish_layer(prod, frc, lhs, fold, wcol, kern, ng)
+    val_up[0:40, :] = val[160:200, :]
+    for a in range(5, 8):
+        load_plane(field_row(a), lhs, (a - 5) * 40)
+    spread_planes(val_up, 40, lhs[0:120, :], spread)
+    for p in range(4):
+        inside_plane(1, p, val_up, p, stiff, prod_up, frc_up)
 
 
 def late_kernel(
     ha, stiff, spread, fold, wcol, kern_low, ng_low, mass, targ, val_up, prod_up, frc_up,
-    ng, own, buf_s, buf_d, buf_sd, kern, g, lhs, val, prod, frc,
+    ng, own, buf_s, buf_d, buf_sd, kern, lhs, val, prod, frc,
 ):
     keep_d = (lax.axis_index("depth") < lax.axis_size("depth") - 1).astype(F32)
     keep_s = (lax.axis_index("surf") < lax.axis_size("surf") - 1).astype(F32)
-    for x in range(8):
-        g[x * 17 : x * 17 + 16, :] = ha[x * 16 : x * 16 + 16, :] * keep_s
-        g[x * 17 + 16 : x * 17 + 17, :] = ha[128 + x : 129 + x, :] * (keep_s * keep_d)
-    load_plane(g, 17, 0, lhs, 0)
-    val[...] = dot2(lhs[0:40, :], spread[...])
+
+    def row_of(c):
+        if c == 16:
+            return ha[128:136, :] * (keep_s * keep_d)
+        return ha[pl.ds(c, 8, stride=16), :] * keep_s
+
+    load_plane(row_of, lhs, 0)
+    spread_planes(val, 0, lhs[0:40, :], spread)
     inside_plane(1, 4, val, 0, stiff, prod, frc)
     across_planes(1, val_up, lambda q, r: val[node_tile(0, q, r)], stiff, prod_up, frc_up, prod, frc)
     finish_layer(prod, frc, lhs, fold, wcol, kern, ng)
@@ -300,7 +342,7 @@
 
 
 def final_kernel(
-    wave, wave_old, adj, adj_old, src, adj_src, inner, near, got_s, got_d, got_sd,
+    fields, wave_old, adj_old, src, adj_src, inner, near, got_s, got_d, got_sd,
     wave_next, adj_next, bricks, wave_buf, adj_buf, brick_buf, sem,
 ):
     keep_s = (lax.axis_index("surf") > 0).astype(F32)
@@ -319,9 +361,11 @@
         scale = (DT * DT) / total(8, a)
         for t in range(4):
             at = slice(t * PLANE + a * 16, t * PLANE + a * 16 + 16)
-            wave_buf[at, :] = 2.0 * wave[at, :] - wave_old[at, :] + (src[at, :] - total(t, a)) * scale
+            now = slice(t * COLUMN + a * 16, t * COLUMN + a * 16 + 16)
+            adj = slice(now.start + 4 * COLUMN, now.stop + 4 * COLUMN)
+            wave_buf[at, :] = 2.0 * fields[now, :] - wave_old[at, :] + (src[at, :] - total(t, a)) * scale
             adj_buf[at, :] = (
-                2.0 * adj[at, :] - adj_old[at, :] + (adj_src[at, :] - total(4 + t, a)) * scale
+                2.0 * fields[adj, :] - adj_old[at, :] + (adj_src[at, :] - total(4 + t, a)) * scale
             )
     copies = [
         pltpu.make_async_copy(wave_buf, wave_next, sem.at[0]),
@@ -396,32 +440,31 @@
     prep = call(
         prep_kernel,
         "prep",
-        [in_hbm(x) for x in (inv_density, inv_modulus, element_cell, send_elem, send_brick)]
-        + [send_count],
-        (out(128, 256), out(160, 128), out(8, 256), out(512, 640, dtype=BF16),
-         out(640, 512, dtype=BF16), out(128, 128)),
+        [in_hbm(x) for x in (wave, adj, inv_density, inv_modulus, element_cell, send_elem, send_brick, send_count)],
+        (out(8 * COLUMN, 128), out(128, 256), out(160, 128), out(8, 256),
+         out(512, 512, dtype=BF16), out(512, 512, dtype=BF16), out(128, 128)),
         [vmem(125, 256), vmem(125, 256), pltpu.VMEM((1, 256), jnp.int32),
          pltpu.VMEM((1, 4, 256), jnp.int32), pltpu.VMEM((1, 4, 256), jnp.int32),
-         pltpu.SemaphoreType.DMA((5,)), vmem(128, 128), vmem(128, 128), vmem(25, 512)],
-        [there] * 5 + [pl.BlockSpec(memory_space=pltpu.SMEM)],
+         pltpu.SMEM((1, 4), jnp.int32), pltpu.SemaphoreType.DMA((14,)), vmem(160, 128), vmem(160, 128), vmem(64, 512)],
+        [there] * 8,
     )
     hc, plane, prep = lax.optimization_barrier((hc, plane, tuple(prep)))
-    stiff, mass, targ, spread, fold, wcol = prep
+    fields, stiff, mass, targ, spread, fold, wcol = prep
     ha = send(jnp.concatenate([plane.reshape(128, 128), hc[:, 0]], 0), -1, 0, True, True)
 
     kern_low, ng_low, val_up, prod_up, frc_up = call(
         early_kernel,
         "early",
-        (wave, adj, hc, stiff, spread, fold, wcol),
+        (fields, hc.reshape(64, 128), stiff, spread, fold, wcol),
         (out(128, 128), out(8 * NROW, 128), out(160, 640), out(800, 128), out(160, 640)),
-        [vmem(8 * NROW, 128), vmem(200, 512), vmem(200, 640), vmem(1000, 128), vmem(200, 640)],
+        [vmem(200, 512), vmem(200, 640), vmem(1000, 128), vmem(200, 640)],
     )
     ng, own, buf_s, buf_d, buf_sd = call(
         late_kernel,
         "late",
         (ha, stiff, spread, fold, wcol, kern_low, ng_low, mass, targ, val_up, prod_up, frc_up),
         (out(8 * NROW, 128), out(256, 128), out(400, 128), out(328, 128), out(272, 128)),
-        [vmem(128, 128), vmem(8 * 17, 128), vmem(200, 512), vmem(40, 640),
+        [vmem(128, 128), vmem(200, 512), vmem(40, 640),
          vmem(1000, 128), vmem(200, 640)],
     )
     got_s = send(buf_s, 1, 0, True, True)
@@ -433,7 +476,7 @@
     wave_next, adj_next, bricks = call(
         final_kernel,
         "final",
-        (wave, wave_old, adj, adj_old, source, adj_source, inner, near, got_s, got_d, got_sd),
+        (fields, wave_old, adj_old, source, adj_source, inner, near, got_s, got_d, got_sd),
         (out(4 * PLANE, 128), out(4 * PLANE, 128), out(125, 1024)),
         [vmem(4 * PLANE, 128), vmem(4 * PLANE, 128), vmem(125, 1024), pltpu.SemaphoreType.DMA((2 + CHUNKS,))],
         out_space=pl.ANY,

time: 28 us -> 27 us (0.964)
  Pallas kernels: 9.46 us -> 8.34 us
  waiting for transfers between devices: 8.33 us -> 9.21 us
  starting transfers between devices: 9.16 us -> 8.43 us
    pallas_call x6, Pallas kernels: 9.46 us -> 8.34 us  [call(): pl.pallas_call(kernel, out_shape=tuple(outs), in_specs=specs or [here] *...]
    ppermute x5, waiting for transfers between devices: 8.33 us -> 9.21 us  [send(): return lax.ppermute(x, ('surf', 'depth'), pairs)]
    ppermute x5, starting transfers between devices: 9.16 us -> 8.43 us  [send(): return lax.ppermute(x, ('surf', 'depth'), pairs)]
  transfers between devices with their start and end apart: 5 -> 5, of which waited for: 3 -> 3; matrix products, arithmetic and copies ran while one was open for 0% -> 0% of each run, Pallas kernels for 21% -> 18%
where the time goes in v3:
time: 27 us; the launch traced here: 26.7 us
  waiting for transfers between devices  9.21 us (34%)
  starting transfers between devices  8.43 us (31%)
  Pallas kernels  8.34 us (31%)
  between operations  0.72 us (3%)
    ppermute x5, waiting for transfers between devices, send(): return lax.ppermute(x, ('surf', 'depth'), pairs)  9.21 us
    ppermute x5, starting transfers between devices, send(): return lax.ppermute(x, ('surf', 'depth'), pairs)  8.43 us
    pallas_call x6, Pallas kernels, call(): pl.pallas_call(kernel, out_shape=tuple(outs), in_specs=specs or [here] *...  8.34 us
  transfers between devices with their start and end apart: 5, of which 3 were waited for; matrix products, arithmetic and copies ran while one was open for 0% of the time, Pallas kernels for 18%

profile of v3, /device:TPU:7, one launch (start us, length us, event | category | flops | bytes accessed | tf_op | source)
XLA Modules:
  0.0 26.7 jit_solution(6633546453281115192)
XLA Ops:
  0.6 0.9 %pack.1 = (f32[8,8,128]{2,1,0:T(8,128)S(1)}, f32[8,16,128]{2,1,0:T(8,128)S(1)}) custom-call(f32[4,8,16,128]{3,2,1,0:T(8,128)} %wave.1, f32[4,8,16,128]{3,2,1,0:T(8,128)} %adj.1), custom_call_target="tpu_custom_call" | custom-call | tf_op jit(solution)/shard_map/pack/pallas_call | solution.py:410
  1.5 0.7 %collective-permute-start = (f32[8,8,128]{2,0,1:T(8,128)S(1)}, f32[8,8,128]{2,0,1:T(8,128)S(1)}, u32[]{:S(2)}, u32[]{:S(2)}) collective-permute-start(f32[8,8,128]{2,0,1:T(8,128)S(1)} %copy.16), channel_id=1, source_target_pairs={{0,7},{1,0},{2,1},{3,2},{4,3},{5,4},{6,5},{7,6},{8,15},{9,8},{10,9... | collective-permute-start | bytes 98312 | tf_op jit(solution)/shard_map/ppermute | solution.py:405
  2.2 2.0 %prep.1 = (f32[1088,128]{1,0:T(8,128)S(1)}, f32[128,256]{1,0:T(8,128)S(1)}, f32[160,128]{1,0:T(8,128)S(1)}, f32[8,256]{1,0:T(8,128)S(1)}, bf16[512,512]{1,0:T(8,...) custom-call(f32[512,128]{1,0:T(8,128)} %bitcast.20, f32[512,128]{1,0:T(8,128)} %bitcast.21, ...), custom_call_target="tpu_custom_call" | custom-call | tf_op jit(solution)/shard_map/prep/pallas_call | solution.py:410
  4.2 1.9 %collective-permute-done = f32[8,8,128]{2,0,1:T(8,128)S(1)} collective-permute-done((f32[8,8,128]{2,0,1:T(8,128)S(1)}, f32[8,8,128]{2,0,1:T(8,128)S(1)}, u32[]{:S(2)}, u32[]{:S(2)}) %collective-permute-start) | collective-permute-done | bytes 32800 | tf_op jit(solution)/shard_map/ppermute | solution.py:405
  6.1 6.3 %collective-permute-start.1 = (f32[136,128]{1,0:T(8,128)S(1)}, f32[136,128]{1,0:T(8,128)S(1)}, u32[]{:S(2)}, u32[]{:S(2)}) collective-permute-start(f32[136,128]{1,0:T(8,128)S(1)} %pad_maximum_fusion), channel_id=1, source_target_pairs={{0,120},{1,121},{2,122},{3,123},{4,124},{5,125},{6,126},{7,127},{8... | collective-permute-start | bytes 208904 | tf_op jit(solution)/shard_map/ppermute | solution.py:405
  12.4 2.1 %early.1 = (f32[128,128]{1,0:T(8,128)S(1)}, f32[680,128]{1,0:T(8,128)S(1)}, f32[160,640]{1,0:T(8,128)S(1)}, f32[800,128]{1,0:T(8,128)S(1)}, f32[160,640]{1,0:T(8,128)S(1)}) custom-call(f32[1088,128]{1,0:T(8,128)S(1)} %get-tuple-element.45.fields, f32[64,128]{1,0:T(8,128)S(1)} %bitcast.18, f32[128,256]{1,0:T(8,128)S(1)} %get-tuple-element.48.stiff, ...), custom_call_target="tpu_custom_call" | custom-call | tf_op jit(solution)/shard_map/early/pallas_call | solution.py:410
  14.4 0.0 collective-permute-done.1.ha
  14.5 1.0 %late.1 = (f32[680,128]{1,0:T(8,128)S(1)}, f32[256,128]{1,0:T(8,128)S(1)}, f32[400,128]{1,0:T(8,128)S(1)}, f32[328,128]{1,0:T(8,128)S(1)}, f32[272,128]{1,0:T(8,128)S(1)}) custom-call(f32[136,128]{1,0:T(8,128)S(1)} %collective-permute-done.1.ha, f32[128,256]{1,0:T(8,128)S(1)} %get-tuple-element.48.stiff, bf16[512,512]{1,0:T(8,128)(2,1)S(1)} %get-tuple-element.49.spread, ...), custom_call_target="tpu_custom_call" | custom-call | tf_op jit(solution)/shard_map/late/pallas_call | solution.py:410
  15.5 0.1 collective-permute-start.3
  15.6 0.7 %collective-permute-start.2 = (f32[328,128]{1,0:T(8,128)S(1)}, f32[328,128]{1,0:T(8,128)S(1)}, u32[]{:S(2)}, u32[]{:S(2)}) collective-permute-start(f32[328,128]{1,0:T(8,128)S(1)} %get-tuple-element.60), channel_id=1, source_target_pairs={{0,1},{1,2},{2,3},{3,4},{4,5},{5,6},{6,7},{7,0},{8,9},{9,10},{10,1... | collective-permute-start | bytes 503816 | tf_op jit(solution)/shard_map/ppermute | solution.py:405
  16.3 0.7 %collective-permute-start.4 = (f32[272,128]{1,0:T(8,128)S(1)}, f32[272,128]{1,0:T(8,128)S(1)}, u32[]{:S(2)}, u32[]{:S(2)}) collective-permute-start(f32[272,128]{1,0:T(8,128)S(1)} %get-tuple-element.65), channel_id=1, source_target_pairs={{0,9},{1,10},{2,11},{3,12},{4,13},{5,14},{6,15},{8,17},{9,18},{10,... | collective-permute-start | bytes 417800 | tf_op jit(solution)/shard_map/ppermute | solution.py:405
  17.0 1.6 %collective-permute-done.2.got_d = f32[328,128]{1,0:T(8,128)S(1)} collective-permute-done((f32[328,128]{1,0:T(8,128)S(1)}, f32[328,128]{1,0:T(8,128)S(1)}, u32[]{:S(2)}, u32[]{:S(2)}) %collective-permute-start.2) | collective-permute-done | bytes 167968 | tf_op jit(solution)/shard_map/ppermute | solution.py:405
  18.6 0.0 copy-start
  18.6 0.0 copy-start.1
  18.6 0.0 copy-start.2
  18.7 0.0 copy-start.3
  18.7 0.7 %near.1 = (f32[128,1024]{1,0:T(8,128)S(1)}, f32[9,8,16,128]{3,2,1,0:T(8,128)S(1)}) custom-call(f32[256,128]{1,0:T(8,128)S(1)} %get-tuple-element.59.own, f32[328,128]{1,0:T(8,128)S(1)} %collective-permute-done.2.got_d, f32[680,128]{1,0:T(8,128)S(1)} %get-tuple-element.53.ng_low, f32[680,128]{1,0:T(8,128)S(1)} %get-tuple-element.61.ng, ...), custom_call_target="tpu_custom_call" | custom-call | tf_op jit(solution)/shard_map/near/pallas_call | solution.py:410
  19.4 0.0 collective-permute-done.4.got_sd
  19.4 5.7 %collective-permute-done.3.got_s = f32[400,128]{1,0:T(8,128)S(1)} collective-permute-done((f32[400,128]{1,0:T(8,128)S(1)}, f32[400,128]{1,0:T(8,128)S(1)}, u32[]{:S(2)}, u32[]{:S(2)}) %collective-permute-start.3) | collective-permute-done | bytes 204832 | tf_op jit(solution)/shard_map/ppermute | solution.py:405
  25.1 0.0 copy-done
  25.1 0.0 copy-done.1
  25.1 0.0 copy-done.2
  25.1 0.0 copy-done.3
  25.1 1.6 %final.1 = (f32[512,128]{1,0:T(8,128)}, f32[512,128]{1,0:T(8,128)}, f32[125,1024]{1,0:T(8,128)}) custom-call(f32[1088,128]{1,0:T(8,128)S(1)} %get-tuple-element.45.fields, f32[512,128]{1,0:T(8,128)S(1)} %bitcast.14, f32[512,128]{1,0:T(8,128)S(1)} %bitcast.15, f32[512,128]{1,0:T(8,128)S(1)} %bitcast.16, f32[512,128]{1,0:T(8,128)S(1)} %bitcast.17, ...), custom_call_target="tpu_custom_call" | custom-call | tf_op jit(solution)/shard_map/final/pallas_call | solution.py:410
  (4 shorter events, 0.0 us)
Async XLA Ops:
  1.5 4.6 %collective-permute-start = (f32[8,8,128]{2,0,1:T(8,128)S(1)}, f32[8,8,128]{2,0,1:T(8,128)S(1)}, u32[]{:S(2)}, u32[]{:S(2)}) collective-permute-start(f32[8,8,128]{2,0,1:T(8,128)S(1)} %copy.16), channel_id=1, source_target_pairs={{0,7},{1,0},{2,1},{3,2},{4,3},{5,4},{6,5},{7,6},{8,15},{9,8},{10,9... | collective-permute-start | bytes 98312 | tf_op jit(solution)/shard_map/ppermute | solution.py:405
  6.1 8.4 %collective-permute-start.1 = (f32[136,128]{1,0:T(8,128)S(1)}, f32[136,128]{1,0:T(8,128)S(1)}, u32[]{:S(2)}, u32[]{:S(2)}) collective-permute-start(f32[136,128]{1,0:T(8,128)S(1)} %pad_maximum_fusion), channel_id=1, source_target_pairs={{0,120},{1,121},{2,122},{3,123},{4,124},{5,125},{6,126},{7,127},{8... | collective-permute-start | bytes 208904 | tf_op jit(solution)/shard_map/ppermute | solution.py:405
  15.5 9.6 %collective-permute-start.3 = (f32[400,128]{1,0:T(8,128)S(1)}, f32[400,128]{1,0:T(8,128)S(1)}, u32[]{:S(2)}, u32[]{:S(2)}) collective-permute-start(f32[400,128]{1,0:T(8,128)S(1)} %get-tuple-element.64), channel_id=1, source_target_pairs={{0,8},{1,9},{2,10},{3,11},{4,12},{5,13},{6,14},{7,15},{8,16},{9,17... | collective-permute-start | bytes 614408 | tf_op jit(solution)/shard_map/ppermute | solution.py:405
  15.6 3.0 %collective-permute-start.2 = (f32[328,128]{1,0:T(8,128)S(1)}, f32[328,128]{1,0:T(8,128)S(1)}, u32[]{:S(2)}, u32[]{:S(2)}) collective-permute-start(f32[328,128]{1,0:T(8,128)S(1)} %get-tuple-element.60), channel_id=1, source_target_pairs={{0,1},{1,2},{2,3},{3,4},{4,5},{5,6},{6,7},{7,0},{8,9},{9,10},{10,1... | collective-permute-start | bytes 503816 | tf_op jit(solution)/shard_map/ppermute | solution.py:405
  16.3 3.0 %collective-permute-start.4 = (f32[272,128]{1,0:T(8,128)S(1)}, f32[272,128]{1,0:T(8,128)S(1)}, u32[]{:S(2)}, u32[]{:S(2)}) collective-permute-start(f32[272,128]{1,0:T(8,128)S(1)} %get-tuple-element.65), channel_id=1, source_target_pairs={{0,9},{1,10},{2,11},{3,12},{4,13},{5,14},{6,15},{8,17},{9,18},{10,... | collective-permute-start | bytes 417800 | tf_op jit(solution)/shard_map/ppermute | solution.py:405
  18.6 6.4 %copy-start = (f32[4,8,16,128]{3,2,1,0:T(8,128)S(1)}, f32[4,8,16,128]{3,2,1,0:T(8,128)}, u32[]{:S(2)}) copy-start(f32[4,8,16,128]{3,2,1,0:T(8,128)} %param.13) | copy-start | bytes 786436
  18.6 6.4 %copy-start.1 = (f32[4,8,16,128]{3,2,1,0:T(8,128)S(1)}, f32[4,8,16,128]{3,2,1,0:T(8,128)}, u32[]{:S(2)}) copy-start(f32[4,8,16,128]{3,2,1,0:T(8,128)} %param.15) | copy-start | bytes 786436
  18.6 6.4 %copy-start.2 = (f32[4,8,16,128]{3,2,1,0:T(8,128)S(1)}, f32[4,8,16,128]{3,2,1,0:T(8,128)}, u32[]{:S(2)}) copy-start(f32[4,8,16,128]{3,2,1,0:T(8,128)} %param.16) | copy-start | bytes 786436
  18.7 6.4 %copy-start.3 = (f32[4,8,16,128]{3,2,1,0:T(8,128)S(1)}, f32[4,8,16,128]{3,2,1,0:T(8,128)}, u32[]{:S(2)}) copy-start(f32[4,8,16,128]{3,2,1,0:T(8,128)} %param.17) | copy-start | bytes 786436

commit v4 on v3

--- a/solution.py
+++ b/solution.py
@@ -316,18 +316,16 @@
     buf_sd[265:272, :] = jnp.zeros((7, 128), F32)
 
 
-def add_bricks(acc, buf, first=0, count=1024):
-    bricks = lax.broadcasted_iota(jnp.int32, (count, 128), 0).astype(F32) + float(first)
-    for ea in range(2):
-        block = buf[ea * 128 : ea * 128 + 128, :]
-        hit = jnp.where(bricks == block[125:126, :], 1.0, 0.0).astype(BF16)
-        term = dot2(block, hit, NT)
-        acc = term if acc is None else acc + term
-    return acc
+def brick_sums(bufs, first=0, count=1024):
+    blocks = jnp.concatenate([buf[at : at + 128, :] for buf in bufs for at in (0, 128)], axis=1)
+    target = blocks[125:126, :]
+    bricks = lax.broadcasted_iota(jnp.int32, (count, blocks.shape[1]), 0).astype(F32) + float(first)
+    hit = jnp.where(bricks == target, 1.0, 0.0).astype(BF16)
+    return dot2(blocks, hit, NT)
 
 
 def near_kernel(own, got_d, ng_low, ng, mass, near, inner):
-    near[...] = add_bricks(add_bricks(None, own), got_d)
+    near[...] = brick_sums((own, got_d))
     for x in range(8):
         for a in range(8):
             low, high = x * NROW + a * 17, x * NROW + (a - 4) * 17
@@ -375,9 +373,7 @@
         c.start()
     for k in range(CHUNKS):
         cols = slice(k * (1024 // CHUNKS), (k + 1) * (1024 // CHUNKS))
-        acc = near[:, cols]
-        for buf in (got_s, got_sd):
-            acc = add_bricks(acc, buf, k * (1024 // CHUNKS), 1024 // CHUNKS)
+        acc = near[:, cols] + brick_sums((got_s, got_sd), k * (1024 // CHUNKS), 1024 // CHUNKS)
         brick_buf[:, cols] = acc[0:125, :]
         copy = pltpu.make_async_copy(brick_buf.at[:, cols], bricks.at[:, cols], sem.at[2 + k])
         copy.start()

time: 27 us -> 26.8 us (level)
  Pallas kernels: 8.34 us -> 7.91 us
    pallas_call x6, Pallas kernels: 8.34 us -> 7.91 us  [call(): pl.pallas_call(kernel, out_shape=tuple(outs), in_specs=specs or [here] *...]
  transfers between devices with their start and end apart: 5 -> 5, of which waited for: 3 -> 3; matrix products, arithmetic and copies ran while one was open for 0% -> 0% of each run, Pallas kernels for 18% -> 17%
where the time goes in v4:
time: 26.8 us; the launch traced here: 26.5 us
  waiting for transfers between devices  9.42 us (35%)
  starting transfers between devices  8.43 us (31%)
  Pallas kernels  7.91 us (30%)
  between operations  0.72 us (3%)
    ppermute x5, waiting for transfers between devices, send(): return lax.ppermute(x, ('surf', 'depth'), pairs)  9.42 us
    ppermute x5, starting transfers between devices, send(): return lax.ppermute(x, ('surf', 'depth'), pairs)  8.43 us
    pallas_call x6, Pallas kernels, call(): pl.pallas_call(kernel, out_shape=tuple(outs), in_specs=specs or [here] *...  7.91 us
  transfers between devices with their start and end apart: 5, of which 3 were waited for; matrix products, arithmetic and copies ran while one was open for 0% of the time, Pallas kernels for 17%

profile of v4, /device:TPU:7, one launch (start us, length us, event | category | flops | bytes accessed | tf_op | source)
XLA Modules:
  0.0 26.5 jit_solution(16000555352939594770)
XLA Ops:
  0.6 0.9 %pack.1 = (f32[8,8,128]{2,1,0:T(8,128)S(1)}, f32[8,16,128]{2,1,0:T(8,128)S(1)}) custom-call(f32[4,8,16,128]{3,2,1,0:T(8,128)} %wave.1, f32[4,8,16,128]{3,2,1,0:T(8,128)} %adj.1), custom_call_target="tpu_custom_call" | custom-call | tf_op jit(solution)/shard_map/pack/pallas_call | solution.py:406
  1.5 0.7 %collective-permute-start = (f32[8,8,128]{2,0,1:T(8,128)S(1)}, f32[8,8,128]{2,0,1:T(8,128)S(1)}, u32[]{:S(2)}, u32[]{:S(2)}) collective-permute-start(f32[8,8,128]{2,0,1:T(8,128)S(1)} %copy.16), channel_id=1, source_target_pairs={{0,7},{1,0},{2,1},{3,2},{4,3},{5,4},{6,5},{7,6},{8,15},{9,8},{10,9... | collective-permute-start | bytes 98312 | tf_op jit(solution)/shard_map/ppermute | solution.py:401
  2.2 2.0 %prep.1 = (f32[1088,128]{1,0:T(8,128)S(1)}, f32[128,256]{1,0:T(8,128)S(1)}, f32[160,128]{1,0:T(8,128)S(1)}, f32[8,256]{1,0:T(8,128)S(1)}, bf16[512,512]{1,0:T(8,...) custom-call(f32[512,128]{1,0:T(8,128)} %bitcast.20, f32[512,128]{1,0:T(8,128)} %bitcast.21, ...), custom_call_target="tpu_custom_call" | custom-call | tf_op jit(solution)/shard_map/prep/pallas_call | solution.py:406
  4.2 1.9 %collective-permute-done = f32[8,8,128]{2,0,1:T(8,128)S(1)} collective-permute-done((f32[8,8,128]{2,0,1:T(8,128)S(1)}, f32[8,8,128]{2,0,1:T(8,128)S(1)}, u32[]{:S(2)}, u32[]{:S(2)}) %collective-permute-start) | collective-permute-done | bytes 32800 | tf_op jit(solution)/shard_map/ppermute | solution.py:401
  6.1 6.3 %collective-permute-start.1 = (f32[136,128]{1,0:T(8,128)S(1)}, f32[136,128]{1,0:T(8,128)S(1)}, u32[]{:S(2)}, u32[]{:S(2)}) collective-permute-start(f32[136,128]{1,0:T(8,128)S(1)} %pad_maximum_fusion), channel_id=1, source_target_pairs={{0,120},{1,121},{2,122},{3,123},{4,124},{5,125},{6,126},{7,127},{8... | collective-permute-start | bytes 208904 | tf_op jit(solution)/shard_map/ppermute | solution.py:401
  12.4 2.1 %early.1 = (f32[128,128]{1,0:T(8,128)S(1)}, f32[680,128]{1,0:T(8,128)S(1)}, f32[160,640]{1,0:T(8,128)S(1)}, f32[800,128]{1,0:T(8,128)S(1)}, f32[160,640]{1,0:T(8,128)S(1)}) custom-call(f32[1088,128]{1,0:T(8,128)S(1)} %get-tuple-element.45.fields, f32[64,128]{1,0:T(8,128)S(1)} %bitcast.18, f32[128,256]{1,0:T(8,128)S(1)} %get-tuple-element.48.stiff, ...), custom_call_target="tpu_custom_call" | custom-call | tf_op jit(solution)/shard_map/early/pallas_call | solution.py:406
  14.4 0.0 collective-permute-done.1.ha
  14.5 1.0 %late.1 = (f32[680,128]{1,0:T(8,128)S(1)}, f32[256,128]{1,0:T(8,128)S(1)}, f32[400,128]{1,0:T(8,128)S(1)}, f32[328,128]{1,0:T(8,128)S(1)}, f32[272,128]{1,0:T(8,128)S(1)}) custom-call(f32[136,128]{1,0:T(8,128)S(1)} %collective-permute-done.1.ha, f32[128,256]{1,0:T(8,128)S(1)} %get-tuple-element.48.stiff, bf16[512,512]{1,0:T(8,128)(2,1)S(1)} %get-tuple-element.49.spread, ...), custom_call_target="tpu_custom_call" | custom-call | tf_op jit(solution)/shard_map/late/pallas_call | solution.py:406
  15.5 0.1 collective-permute-start.3
  15.6 0.7 %collective-permute-start.2 = (f32[328,128]{1,0:T(8,128)S(1)}, f32[328,128]{1,0:T(8,128)S(1)}, u32[]{:S(2)}, u32[]{:S(2)}) collective-permute-start(f32[328,128]{1,0:T(8,128)S(1)} %get-tuple-element.60), channel_id=1, source_target_pairs={{0,1},{1,2},{2,3},{3,4},{4,5},{5,6},{6,7},{7,0},{8,9},{9,10},{10,1... | collective-permute-start | bytes 503816 | tf_op jit(solution)/shard_map/ppermute | solution.py:401
  16.3 0.7 %collective-permute-start.4 = (f32[272,128]{1,0:T(8,128)S(1)}, f32[272,128]{1,0:T(8,128)S(1)}, u32[]{:S(2)}, u32[]{:S(2)}) collective-permute-start(f32[272,128]{1,0:T(8,128)S(1)} %get-tuple-element.65), channel_id=1, source_target_pairs={{0,9},{1,10},{2,11},{3,12},{4,13},{5,14},{6,15},{8,17},{9,18},{10,... | collective-permute-start | bytes 417800 | tf_op jit(solution)/shard_map/ppermute | solution.py:401
  17.0 1.6 %collective-permute-done.2.got_d = f32[328,128]{1,0:T(8,128)S(1)} collective-permute-done((f32[328,128]{1,0:T(8,128)S(1)}, f32[328,128]{1,0:T(8,128)S(1)}, u32[]{:S(2)}, u32[]{:S(2)}) %collective-permute-start.2) | collective-permute-done | bytes 167968 | tf_op jit(solution)/shard_map/ppermute | solution.py:401
  18.6 0.0 copy-start
  18.6 0.0 copy-start.1
  18.6 0.0 copy-start.2
  18.7 0.0 copy-start.3
  18.7 0.5 %near.1 = (f32[128,1024]{1,0:T(8,128)S(1)}, f32[9,8,16,128]{3,2,1,0:T(8,128)S(1)}) custom-call(f32[256,128]{1,0:T(8,128)S(1)} %get-tuple-element.59.own, f32[328,128]{1,0:T(8,128)S(1)} %collective-permute-done.2.got_d, f32[680,128]{1,0:T(8,128)S(1)} %get-tuple-element.53.ng_low, f32[680,128]{1,0:T(8,128)S(1)} %get-tuple-element.61.ng, ...), custom_call_target="tpu_custom_call" | custom-call | tf_op jit(solution)/shard_map/near/pallas_call | solution.py:406
  19.2 0.0 collective-permute-done.4.got_sd
  19.2 5.9 %collective-permute-done.3.got_s = f32[400,128]{1,0:T(8,128)S(1)} collective-permute-done((f32[400,128]{1,0:T(8,128)S(1)}, f32[400,128]{1,0:T(8,128)S(1)}, u32[]{:S(2)}, u32[]{:S(2)}) %collective-permute-start.3) | collective-permute-done | bytes 204832 | tf_op jit(solution)/shard_map/ppermute | solution.py:401
  25.1 0.0 copy-done
  25.1 0.0 copy-done.1
  25.1 0.0 copy-done.2
  25.1 0.0 copy-done.3
  25.1 1.4 %final.1 = (f32[512,128]{1,0:T(8,128)}, f32[512,128]{1,0:T(8,128)}, f32[125,1024]{1,0:T(8,128)}) custom-call(f32[1088,128]{1,0:T(8,128)S(1)} %get-tuple-element.45.fields, f32[512,128]{1,0:T(8,128)S(1)} %bitcast.14, f32[512,128]{1,0:T(8,128)S(1)} %bitcast.15, f32[512,128]{1,0:T(8,128)S(1)} %bitcast.16, f32[512,128]{1,0:T(8,128)S(1)} %bitcast.17, ...), custom_call_target="tpu_custom_call" | custom-call | tf_op jit(solution)/shard_map/final/pallas_call | solution.py:406
  (4 shorter events, 0.0 us)
Async XLA Ops:
  1.5 4.6 %collective-permute-start = (f32[8,8,128]{2,0,1:T(8,128)S(1)}, f32[8,8,128]{2,0,1:T(8,128)S(1)}, u32[]{:S(2)}, u32[]{:S(2)}) collective-permute-start(f32[8,8,128]{2,0,1:T(8,128)S(1)} %copy.16), channel_id=1, source_target_pairs={{0,7},{1,0},{2,1},{3,2},{4,3},{5,4},{6,5},{7,6},{8,15},{9,8},{10,9... | collective-permute-start | bytes 98312 | tf_op jit(solution)/shard_map/ppermute | solution.py:401
  6.1 8.4 %collective-permute-start.1 = (f32[136,128]{1,0:T(8,128)S(1)}, f32[136,128]{1,0:T(8,128)S(1)}, u32[]{:S(2)}, u32[]{:S(2)}) collective-permute-start(f32[136,128]{1,0:T(8,128)S(1)} %pad_maximum_fusion), channel_id=1, source_target_pairs={{0,120},{1,121},{2,122},{3,123},{4,124},{5,125},{6,126},{7,127},{8... | collective-permute-start | bytes 208904 | tf_op jit(solution)/shard_map/ppermute | solution.py:401
  15.5 9.6 %collective-permute-start.3 = (f32[400,128]{1,0:T(8,128)S(1)}, f32[400,128]{1,0:T(8,128)S(1)}, u32[]{:S(2)}, u32[]{:S(2)}) collective-permute-start(f32[400,128]{1,0:T(8,128)S(1)} %get-tuple-element.64), channel_id=1, source_target_pairs={{0,8},{1,9},{2,10},{3,11},{4,12},{5,13},{6,14},{7,15},{8,16},{9,17... | collective-permute-start | bytes 614408 | tf_op jit(solution)/shard_map/ppermute | solution.py:401
  15.6 3.0 %collective-permute-start.2 = (f32[328,128]{1,0:T(8,128)S(1)}, f32[328,128]{1,0:T(8,128)S(1)}, u32[]{:S(2)}, u32[]{:S(2)}) collective-permute-start(f32[328,128]{1,0:T(8,128)S(1)} %get-tuple-element.60), channel_id=1, source_target_pairs={{0,1},{1,2},{2,3},{3,4},{4,5},{5,6},{6,7},{7,0},{8,9},{9,10},{10,1... | collective-permute-start | bytes 503816 | tf_op jit(solution)/shard_map/ppermute | solution.py:401
  16.3 2.8 %collective-permute-start.4 = (f32[272,128]{1,0:T(8,128)S(1)}, f32[272,128]{1,0:T(8,128)S(1)}, u32[]{:S(2)}, u32[]{:S(2)}) collective-permute-start(f32[272,128]{1,0:T(8,128)S(1)} %get-tuple-element.65), channel_id=1, source_target_pairs={{0,9},{1,10},{2,11},{3,12},{4,13},{5,14},{6,15},{8,17},{9,18},{10,... | collective-permute-start | bytes 417800 | tf_op jit(solution)/shard_map/ppermute | solution.py:401
  18.6 6.4 %copy-start = (f32[4,8,16,128]{3,2,1,0:T(8,128)S(1)}, f32[4,8,16,128]{3,2,1,0:T(8,128)}, u32[]{:S(2)}) copy-start(f32[4,8,16,128]{3,2,1,0:T(8,128)} %param.13) | copy-start | bytes 786436
  18.6 6.4 %copy-start.1 = (f32[4,8,16,128]{3,2,1,0:T(8,128)S(1)}, f32[4,8,16,128]{3,2,1,0:T(8,128)}, u32[]{:S(2)}) copy-start(f32[4,8,16,128]{3,2,1,0:T(8,128)} %param.15) | copy-start | bytes 786436
  18.6 6.4 %copy-start.2 = (f32[4,8,16,128]{3,2,1,0:T(8,128)S(1)}, f32[4,8,16,128]{3,2,1,0:T(8,128)}, u32[]{:S(2)}) copy-start(f32[4,8,16,128]{3,2,1,0:T(8,128)} %param.16) | copy-start | bytes 786436
  18.7 6.4 %copy-start.3 = (f32[4,8,16,128]{3,2,1,0:T(8,128)S(1)}, f32[4,8,16,128]{3,2,1,0:T(8,128)}, u32[]{:S(2)}) copy-start(f32[4,8,16,128]{3,2,1,0:T(8,128)} %param.17) | copy-start | bytes 786436

commit v5 on v4

--- a/solution.py
+++ b/solution.py
@@ -324,58 +324,83 @@
     return dot2(blocks, hit, NT)
 
 
-def near_kernel(own, got_d, ng_low, ng, mass, near, inner):
+def stepped(now, before, src, force, scale):
+    return 2.0 * now - before + (src - force) * scale
+
+
+def near_kernel(
+    own, got_d, ng_low, ng, mass, fields, wave_old, adj_old, src, adj_src,
+    near, edge, wave_next, adj_next, wave_buf, adj_buf, sem,
+):
+    keep_d = (lax.axis_index("depth") > 0).astype(F32)
+    first = lax.broadcasted_iota(jnp.int32, (16, 128), 0) == 0
+
+    def total(ch, a):
+        if ch == 8:
+            part = mass[a * 17 : a * 17 + 16, :]
+        else:
+            low, high = ch * NROW + a * 17, ch * NROW + (a - 4) * 17
+            part = ng_low[low : low + 16, :] if a <= 4 else ng[high : high + 16, :]
+            if a == 4:
+                part = part + ng[high : high + 16, :]
+        line = got_d[256 + ch * 8 + a : 257 + ch * 8 + a, :] * keep_d
+        return part + jnp.where(first, line, 0.0)
+
+    for ch in range(9):
+        edge[ch] = total(ch, 0)
+    for a in range(1, 8):
+        scale = (DT * DT) / total(8, a)
+        for t in range(4):
+            at = slice(t * PLANE + a * 16, t * PLANE + a * 16 + 16)
+            now = slice(t * COLUMN + a * 16, t * COLUMN + a * 16 + 16)
+            adj = slice(now.start + 4 * COLUMN, now.stop + 4 * COLUMN)
+            wave_buf[at, :] = stepped(fields[now, :], wave_old[at, :], src[at, :], total(t, a), scale)
+            adj_buf[at, :] = stepped(
+                fields[adj, :], adj_old[at, :], adj_src[at, :], total(4 + t, a), scale
+            )
+    copies = []
+    for t in range(4):
+        rows = pl.ds(t * PLANE + 16, PLANE - 16)
+        for k, (buf, to) in enumerate(((wave_buf, wave_next), (adj_buf, adj_next))):
+            copies.append(pltpu.make_async_copy(buf.at[rows], to.at[rows], sem.at[2 * t + k]))
+    for c in copies:
+        c.start()
     near[...] = brick_sums((own, got_d))
-    for x in range(8):
-        for a in range(8):
-            low, high = x * NROW + a * 17, x * NROW + (a - 4) * 17
-            if a < 4:
-                inner[x, a] = ng_low[low : low + 16, :]
-            elif a == 4:
-                inner[x, a] = ng_low[low : low + 16, :] + ng[high : high + 16, :]
-            else:
-                inner[x, a] = ng[high : high + 16, :]
-    for a in range(8):
-        inner[8, a] = mass[a * 17 : a * 17 + 16, :]
+    for c in copies:
+        c.wait()
 
 
 def final_kernel(
-    fields, wave_old, adj_old, src, adj_src, inner, near, got_s, got_d, got_sd,
+    fields, wave_old, adj_old, src, adj_src, edge, near, got_s, got_sd, wave_in, adj_in,
     wave_next, adj_next, bricks, wave_buf, adj_buf, brick_buf, sem,
 ):
     keep_s = (lax.axis_index("surf") > 0).astype(F32)
     keep_d = (lax.axis_index("depth") > 0).astype(F32)
     first = lax.broadcasted_iota(jnp.int32, (16, 128), 0) == 0
 
-    def total(ch, a):
-        part = inner[ch, a]
-        line = got_d[256 + ch * 8 + a : 257 + ch * 8 + a, :] * keep_d
-        if a == 0:
-            part = part + got_s[256 + ch * 16 : 272 + ch * 16, :] * keep_s
-            line = line + got_sd[256 + ch : 257 + ch, :] * (keep_s * keep_d)
-        return part + jnp.where(first, line, 0.0)
-
-    for a in range(8):
-        scale = (DT * DT) / total(8, a)
-        for t in range(4):
-            at = slice(t * PLANE + a * 16, t * PLANE + a * 16 + 16)
-            now = slice(t * COLUMN + a * 16, t * COLUMN + a * 16 + 16)
-            adj = slice(now.start + 4 * COLUMN, now.stop + 4 * COLUMN)
-            wave_buf[at, :] = 2.0 * fields[now, :] - wave_old[at, :] + (src[at, :] - total(t, a)) * scale
-            adj_buf[at, :] = (
-                2.0 * fields[adj, :] - adj_old[at, :] + (adj_src[at, :] - total(4 + t, a)) * scale
-            )
-    copies = [
-        pltpu.make_async_copy(wave_buf, wave_next, sem.at[0]),
-        pltpu.make_async_copy(adj_buf, adj_next, sem.at[1]),
-    ]
+    def total(ch):
+        line = got_sd[256 + ch : 257 + ch, :] * (keep_s * keep_d)
+        plane = got_s[256 + ch * 16 : 272 + ch * 16, :] * keep_s
+        return edge[ch] + plane + jnp.where(first, line, 0.0)
+
+    scale = (DT * DT) / total(8)
+    copies = []
+    for t in range(4):
+        at = slice(t * PLANE, t * PLANE + 16)
+        now = slice(t * COLUMN, t * COLUMN + 16)
+        adj = slice(now.start + 4 * COLUMN, now.stop + 4 * COLUMN)
+        wave_buf[t] = stepped(fields[now, :], wave_old[at, :], src[at, :], total(t), scale)
+        adj_buf[t] = stepped(fields[adj, :], adj_old[at, :], adj_src[at, :], total(4 + t), scale)
+        rows = pl.ds(t * PLANE, 16)
+        for k, (buf, to) in enumerate(((wave_buf, wave_next), (adj_buf, adj_next))):
+            copies.append(pltpu.make_async_copy(buf.at[t], to.at[rows], sem.at[2 * t + k]))
     for c in copies:
         c.start()
     for k in range(CHUNKS):
         cols = slice(k * (1024 // CHUNKS), (k + 1) * (1024 // CHUNKS))
         acc = near[:, cols] + brick_sums((got_s, got_sd), k * (1024 // CHUNKS), 1024 // CHUNKS)
         brick_buf[:, cols] = acc[0:125, :]
-        copy = pltpu.make_async_copy(brick_buf.at[:, cols], bricks.at[:, cols], sem.at[2 + k])
+        copy = pltpu.make_async_copy(brick_buf.at[:, cols], bricks.at[:, cols], sem.at[8 + k])
         copy.start()
         copies.append(copy)
     for c in copies:
@@ -401,14 +426,16 @@
     return lax.ppermute(x, ("surf", "depth"), pairs)
 
 
-def call(kernel, name, ins, outs, scratch=(), specs=None, out_space=pltpu.VMEM):
+def call(kernel, name, ins, outs, scratch=(), specs=None, out_spaces=None, aliases=()):
     here = pl.BlockSpec(memory_space=pltpu.VMEM)
+    spaces = out_spaces or [pltpu.VMEM] * len(outs)
     return pl.pallas_call(
         kernel,
         out_shape=tuple(outs),
         in_specs=specs or [here] * len(ins),
-        out_specs=tuple(pl.BlockSpec(memory_space=out_space) for _ in outs),
+        out_specs=tuple(pl.BlockSpec(memory_space=space) for space in spaces),
         scratch_shapes=list(scratch),
+        input_output_aliases=dict(aliases),
         compiler_params=pltpu.CompilerParams(vmem_limit_bytes=48 * 1024 * 1024),
         name=name,
     )(*ins)
@@ -466,16 +493,25 @@
     got_s = send(buf_s, 1, 0, True, True)
     got_d = send(buf_d, 0, 1, True, True)
     got_sd = send(buf_sd, 1, 1, False, False)
-    near, inner = call(
-        near_kernel, "near", (own, got_d, ng_low, ng, mass), (out(128, 1024), out(9, 8, 16, 128))
+    field = out(4 * PLANE, 128)
+    rest = (fields, wave_old, adj_old, source, adj_source)
+    near, edge, wave_part, adj_part = call(
+        near_kernel,
+        "near",
+        (own, got_d, ng_low, ng, mass) + rest,
+        (out(128, 1024), out(9, 16, 128), field, field),
+        [vmem(4 * PLANE, 128), vmem(4 * PLANE, 128), pltpu.SemaphoreType.DMA((8,))],
+        out_spaces=[pltpu.VMEM, pltpu.VMEM, pltpu.HBM, pltpu.HBM],
     )
     wave_next, adj_next, bricks = call(
         final_kernel,
         "final",
-        (fields, wave_old, adj_old, source, adj_source, inner, near, got_s, got_d, got_sd),
-        (out(4 * PLANE, 128), out(4 * PLANE, 128), out(125, 1024)),
-        [vmem(4 * PLANE, 128), vmem(4 * PLANE, 128), vmem(125, 1024), pltpu.SemaphoreType.DMA((2 + CHUNKS,))],
-        out_space=pl.ANY,
+        rest + (edge, near, got_s, got_sd, wave_part, adj_part),
+        (field, field, out(125, 1024)),
+        [vmem(4, 16, 128), vmem(4, 16, 128), vmem(125, 1024), pltpu.SemaphoreType.DMA((8 + CHUNKS,))],
+        [pl.BlockSpec(memory_space=pltpu.VMEM)] * 9 + [there] * 2,
+        [pltpu.HBM, pltpu.HBM, pl.ANY],
+        ((9, 0), (10, 1)),
     )
     return wave_next.reshape(shape), adj_next.reshape(shape), bricks
 

time: 26.8 us -> 26.6 us (level)
  waiting for transfers between devices: 9.42 us -> 8.5 us
  Pallas kernels: 7.91 us -> 8.67 us
    ppermute x5, waiting for transfers between devices: 9.42 us -> 8.5 us  [send(): return lax.ppermute(x, ('surf', 'depth'), pairs)]
    pallas_call x6, Pallas kernels: 7.91 us -> 8.67 us  [call(): pl.pallas_call(kernel, out_shape=tuple(outs), in_specs=specs or [here] *...]
  transfers between devices with their start and end apart: 5 -> 5, of which waited for: 3 -> 3; matrix products, arithmetic and copies ran while one was open for 0% -> 0% of each run, Pallas kernels for 17% -> 21%
where the time goes in v5:
time: 26.6 us; the launch traced here: 26.4 us
  Pallas kernels  8.67 us (33%)
  waiting for transfers between devices  8.5 us (32%)
  starting transfers between devices  8.42 us (32%)
  between operations  0.75 us (3%)
    pallas_call x6, Pallas kernels, call(): pl.pallas_call(kernel, out_shape=tuple(outs), in_specs=specs or [here] *...  8.67 us
    ppermute x5, waiting for transfers between devices, send(): return lax.ppermute(x, ('surf', 'depth'), pairs)  8.5 us
    ppermute x5, starting transfers between devices, send(): return lax.ppermute(x, ('surf', 'depth'), pairs)  8.42 us
  transfers between devices with their start and end apart: 5, of which 3 were waited for; matrix products, arithmetic and copies ran while one was open for 0% of the time, Pallas kernels for 21%

profile of v5, /device:TPU:7, one launch (start us, length us, event | category | flops | bytes accessed | tf_op | source)
XLA Modules:
  0.0 26.4 jit_solution(9116168278187073843)
XLA Ops:
  0.6 0.9 %pack.1 = (f32[8,8,128]{2,1,0:T(8,128)S(1)}, f32[8,16,128]{2,1,0:T(8,128)S(1)}) custom-call(f32[4,8,16,128]{3,2,1,0:T(8,128)} %wave.1, f32[4,8,16,128]{3,2,1,0:T(8,128)} %adj.1), custom_call_target="tpu_custom_call" | custom-call | tf_op jit(solution)/shard_map/pack/pallas_call | solution.py:432
  1.5 0.7 %collective-permute-start = (f32[8,8,128]{2,0,1:T(8,128)S(1)}, f32[8,8,128]{2,0,1:T(8,128)S(1)}, u32[]{:S(2)}, u32[]{:S(2)}) collective-permute-start(f32[8,8,128]{2,0,1:T(8,128)S(1)} %copy.18), channel_id=1, source_target_pairs={{0,7},{1,0},{2,1},{3,2},{4,3},{5,4},{6,5},{7,6},{8,15},{9,8},{10,9... | collective-permute-start | bytes 98312 | tf_op jit(solution)/shard_map/ppermute | solution.py:426
  2.2 2.0 %prep.1 = (f32[1088,128]{1,0:T(8,128)S(1)}, f32[128,256]{1,0:T(8,128)S(1)}, f32[160,128]{1,0:T(8,128)S(1)}, f32[8,256]{1,0:T(8,128)S(1)}, bf16[512,512]{1,0:T(8,...) custom-call(f32[512,128]{1,0:T(8,128)} %bitcast.24, f32[512,128]{1,0:T(8,128)} %bitcast.25, ...), custom_call_target="tpu_custom_call" | custom-call | tf_op jit(solution)/shard_map/prep/pallas_call | solution.py:432
  4.2 1.9 %collective-permute-done = f32[8,8,128]{2,0,1:T(8,128)S(1)} collective-permute-done((f32[8,8,128]{2,0,1:T(8,128)S(1)}, f32[8,8,128]{2,0,1:T(8,128)S(1)}, u32[]{:S(2)}, u32[]{:S(2)}) %collective-permute-start) | collective-permute-done | bytes 32800 | tf_op jit(solution)/shard_map/ppermute | solution.py:426
  6.1 6.3 %collective-permute-start.1 = (f32[136,128]{1,0:T(8,128)S(1)}, f32[136,128]{1,0:T(8,128)S(1)}, u32[]{:S(2)}, u32[]{:S(2)}) collective-permute-start(f32[136,128]{1,0:T(8,128)S(1)} %pad_maximum_fusion), channel_id=1, source_target_pairs={{0,120},{1,121},{2,122},{3,123},{4,124},{5,125},{6,126},{7,127},{8... | collective-permute-start | bytes 208904 | tf_op jit(solution)/shard_map/ppermute | solution.py:426
  12.4 2.1 %early.1 = (f32[128,128]{1,0:T(8,128)S(1)}, f32[680,128]{1,0:T(8,128)S(1)}, f32[160,640]{1,0:T(8,128)S(1)}, f32[800,128]{1,0:T(8,128)S(1)}, f32[160,640]{1,0:T(8,128)S(1)}) custom-call(f32[1088,128]{1,0:T(8,128)S(1)} %get-tuple-element.47.fields, f32[64,128]{1,0:T(8,128)S(1)} %bitcast.22, f32[128,256]{1,0:T(8,128)S(1)} %get-tuple-element.50.stiff, ...), custom_call_target="tpu_custom_call" | custom-call | tf_op jit(solution)/shard_map/early/pallas_call | solution.py:432
  14.5 0.0 collective-permute-done.1.ha
  14.5 0.0 copy-start
  14.5 0.0 copy-start.1
  14.5 0.0 copy-start.2
  14.5 0.0 copy-start.3
  14.5 1.1 %late.1 = (f32[680,128]{1,0:T(8,128)S(1)}, f32[256,128]{1,0:T(8,128)S(1)}, f32[400,128]{1,0:T(8,128)S(1)}, f32[328,128]{1,0:T(8,128)S(1)}, f32[272,128]{1,0:T(8,128)S(1)}) custom-call(f32[136,128]{1,0:T(8,128)S(1)} %collective-permute-done.1.ha, f32[128,256]{1,0:T(8,128)S(1)} %get-tuple-element.50.stiff, bf16[512,512]{1,0:T(8,128)(2,1)S(1)} %get-tuple-element.51.spread, ...), custom_call_target="tpu_custom_call" | custom-call | tf_op jit(solution)/shard_map/late/pallas_call | solution.py:432
  15.6 0.1 collective-permute-start.3
  15.7 0.7 %collective-permute-start.2 = (f32[328,128]{1,0:T(8,128)S(1)}, f32[328,128]{1,0:T(8,128)S(1)}, u32[]{:S(2)}, u32[]{:S(2)}) collective-permute-start(f32[328,128]{1,0:T(8,128)S(1)} %get-tuple-element.62), channel_id=1, source_target_pairs={{0,1},{1,2},{2,3},{3,4},{4,5},{5,6},{6,7},{7,0},{8,9},{9,10},{10,1... | collective-permute-start | bytes 503816 | tf_op jit(solution)/shard_map/ppermute | solution.py:426
  16.4 0.7 %collective-permute-start.4 = (f32[272,128]{1,0:T(8,128)S(1)}, f32[272,128]{1,0:T(8,128)S(1)}, u32[]{:S(2)}, u32[]{:S(2)}) collective-permute-start(f32[272,128]{1,0:T(8,128)S(1)} %get-tuple-element.67), channel_id=1, source_target_pairs={{0,9},{1,10},{2,11},{3,12},{4,13},{5,14},{6,15},{8,17},{9,18},{10,... | collective-permute-start | bytes 417800 | tf_op jit(solution)/shard_map/ppermute | solution.py:426
  17.1 1.6 %collective-permute-done.2.got_d = f32[328,128]{1,0:T(8,128)S(1)} collective-permute-done((f32[328,128]{1,0:T(8,128)S(1)}, f32[328,128]{1,0:T(8,128)S(1)}, u32[]{:S(2)}, u32[]{:S(2)}) %collective-permute-start.2) | collective-permute-done | bytes 167968 | tf_op jit(solution)/shard_map/ppermute | solution.py:426
  18.7 0.0 copy-done
  18.7 0.0 copy-done.1
  18.7 0.0 copy-done.2
  18.7 0.0 copy-done.3
  18.7 1.4 %near.1 = (f32[128,1024]{1,0:T(8,128)S(1)}, f32[9,16,128]{2,1,0:T(8,128)S(1)}, f32[512,128]{1,0:T(8,128)}, f32[512,128]{1,0:T(8,128)}) custom-call(f32[256,128]{1,0:T(8,128)S(1)} %get-tuple-element.61.own, f32[328,128]{1,0:T(8,128)S(1)} %collective-permute-done.2.got_d, f32[680,128]{1,0:T(8,128)S(1)} %get-tuple-element.55.ng_low, ...), custom_call_target="tpu_custom_call" | custom-call | tf_op jit(solution)/shard_map/near/pallas_call | solution.py:432
  20.1 0.0 collective-permute-done.4.got_sd
  20.1 5.0 %collective-permute-done.3.got_s = f32[400,128]{1,0:T(8,128)S(1)} collective-permute-done((f32[400,128]{1,0:T(8,128)S(1)}, f32[400,128]{1,0:T(8,128)S(1)}, u32[]{:S(2)}, u32[]{:S(2)}) %collective-permute-start.3) | collective-permute-done | bytes 204832 | tf_op jit(solution)/shard_map/ppermute | solution.py:426
  25.1 1.3 %final.1 = (f32[512,128]{1,0:T(8,128)}, f32[512,128]{1,0:T(8,128)}, f32[125,1024]{1,0:T(8,128)}) custom-call(f32[1088,128]{1,0:T(8,128)S(1)} %get-tuple-element.47.fields, f32[512,128]{1,0:T(8,128)S(1)} %bitcast.15, f32[512,128]{1,0:T(8,128)S(1)} %bitcast.17, f32[512,128]{1,0:T(8,128)S(1)} %bitcast.19, ...), custom_call_target="tpu_custom_call", output_to_operand_aliasing={{0}: (9, {}), {1}: (10, {})} | custom-call | tf_op jit(solution)/shard_map/final/pallas_call | solution.py:432
  (4 shorter events, 0.0 us)
Async XLA Ops:
  1.5 4.6 %collective-permute-start = (f32[8,8,128]{2,0,1:T(8,128)S(1)}, f32[8,8,128]{2,0,1:T(8,128)S(1)}, u32[]{:S(2)}, u32[]{:S(2)}) collective-permute-start(f32[8,8,128]{2,0,1:T(8,128)S(1)} %copy.18), channel_id=1, source_target_pairs={{0,7},{1,0},{2,1},{3,2},{4,3},{5,4},{6,5},{7,6},{8,15},{9,8},{10,9... | collective-permute-start | bytes 98312 | tf_op jit(solution)/shard_map/ppermute | solution.py:426
  6.1 8.4 %collective-permute-start.1 = (f32[136,128]{1,0:T(8,128)S(1)}, f32[136,128]{1,0:T(8,128)S(1)}, u32[]{:S(2)}, u32[]{:S(2)}) collective-permute-start(f32[136,128]{1,0:T(8,128)S(1)} %pad_maximum_fusion), channel_id=1, source_target_pairs={{0,120},{1,121},{2,122},{3,123},{4,124},{5,125},{6,126},{7,127},{8... | collective-permute-start | bytes 208904 | tf_op jit(solution)/shard_map/ppermute | solution.py:426
  14.5 4.2 %copy-start = (f32[4,8,16,128]{3,2,1,0:T(8,128)S(1)}, f32[4,8,16,128]{3,2,1,0:T(8,128)}, u32[]{:S(2)}) copy-start(f32[4,8,16,128]{3,2,1,0:T(8,128)} %param.13) | copy-start | bytes 786436
  14.5 4.2 %copy-start.1 = (f32[4,8,16,128]{3,2,1,0:T(8,128)S(1)}, f32[4,8,16,128]{3,2,1,0:T(8,128)}, u32[]{:S(2)}) copy-start(f32[4,8,16,128]{3,2,1,0:T(8,128)} %param.15) | copy-start | bytes 786436
  14.5 4.2 %copy-start.2 = (f32[4,8,16,128]{3,2,1,0:T(8,128)S(1)}, f32[4,8,16,128]{3,2,1,0:T(8,128)}, u32[]{:S(2)}) copy-start(f32[4,8,16,128]{3,2,1,0:T(8,128)} %param.16) | copy-start | bytes 786436
  14.5 4.2 %copy-start.3 = (f32[4,8,16,128]{3,2,1,0:T(8,128)S(1)}, f32[4,8,16,128]{3,2,1,0:T(8,128)}, u32[]{:S(2)}) copy-start(f32[4,8,16,128]{3,2,1,0:T(8,128)} %param.17) | copy-start | bytes 786436
  15.6 9.5 %collective-permute-start.3 = (f32[400,128]{1,0:T(8,128)S(1)}, f32[400,128]{1,0:T(8,128)S(1)}, u32[]{:S(2)}, u32[]{:S(2)}) collective-permute-start(f32[400,128]{1,0:T(8,128)S(1)} %get-tuple-element.66), channel_id=1, source_target_pairs={{0,8},{1,9},{2,10},{3,11},{4,12},{5,13},{6,14},{7,15},{8,16},{9,17... | collective-permute-start | bytes 614408 | tf_op jit(solution)/shard_map/ppermute | solution.py:426
  15.7 3.0 %collective-permute-start.2 = (f32[328,128]{1,0:T(8,128)S(1)}, f32[328,128]{1,0:T(8,128)S(1)}, u32[]{:S(2)}, u32[]{:S(2)}) collective-permute-start(f32[328,128]{1,0:T(8,128)S(1)} %get-tuple-element.62), channel_id=1, source_target_pairs={{0,1},{1,2},{2,3},{3,4},{4,5},{5,6},{6,7},{7,0},{8,9},{9,10},{10,1... | collective-permute-start | bytes 503816 | tf_op jit(solution)/shard_map/ppermute | solution.py:426
  16.4 3.7 %collective-permute-start.4 = (f32[272,128]{1,0:T(8,128)S(1)}, f32[272,128]{1,0:T(8,128)S(1)}, u32[]{:S(2)}, u32[]{:S(2)}) collective-permute-start(f32[272,128]{1,0:T(8,128)S(1)} %get-tuple-element.67), channel_id=1, source_target_pairs={{0,9},{1,10},{2,11},{3,12},{4,13},{5,14},{6,15},{8,17},{9,18},{10,... | collective-permute-start | bytes 417800 | tf_op jit(solution)/shard_map/ppermute | solution.py:426

commit v6 on v5

--- a/solution.py
+++ b/solution.py
@@ -276,7 +276,7 @@
 
 def late_kernel(
     ha, stiff, spread, fold, wcol, kern_low, ng_low, mass, targ, val_up, prod_up, frc_up,
-    ng, own, buf_s, buf_d, buf_sd, kern, lhs, val, prod, frc,
+    ng, kern, buf_s, lhs, val, prod, frc,
 ):
     keep_d = (lax.axis_index("depth") < lax.axis_size("depth") - 1).astype(F32)
     keep_s = (lax.axis_index("surf") < lax.axis_size("surf") - 1).astype(F32)
@@ -291,7 +291,18 @@
     inside_plane(1, 4, val, 0, stiff, prod, frc)
     across_planes(1, val_up, lambda q, r: val[node_tile(0, q, r)], stiff, prod_up, frc_up, prod, frc)
     finish_layer(prod, frc, lhs, fold, wcol, kern, ng)
-    for row, buf in ((0, own), (1, buf_s), (2, buf_d), (3, buf_sd)):
+    buf_s[0:128, :] = kern_low[...]
+    buf_s[128:256, :] = kern[...]
+    buf_s[125:126, :] = targ[1:2, 0:128]
+    buf_s[253:254, :] = targ[1:2, 128:256]
+    for x in range(8):
+        base = x * NROW
+        buf_s[256 + x * 16 : 272 + x * 16, :] = ng[base + 68 : base + 84, :]
+    buf_s[384:400, :] = mass[136:152, :]
+
+
+def pick_kernel(kern_low, kern, ng_low, ng, mass, targ, own, buf_d, buf_sd):
+    for row, buf in ((0, own), (2, buf_d), (3, buf_sd)):
         buf[0:128, :] = kern_low[...]
         buf[128:256, :] = kern[...]
         buf[125:126, :] = targ[row : row + 1, 0:128]
@@ -307,11 +318,9 @@
             else:
                 row = ng[at - 68 : at - 67, :]
             buf_d[256 + x * 8 + a : 257 + x * 8 + a, :] = row
-        buf_s[256 + x * 16 : 272 + x * 16, :] = ng[base + 68 : base + 84, :]
         buf_sd[256 + x : 257 + x, :] = ng[base + 84 : base + 85, :]
     for a in range(8):
         buf_d[320 + a : 321 + a, :] = mass[a * 17 + 16 : a * 17 + 17, :]
-    buf_s[384:400, :] = mass[136:152, :]
     buf_sd[264:265, :] = mass[152:153, :]
     buf_sd[265:272, :] = jnp.zeros((7, 128), F32)
 
@@ -482,15 +491,21 @@
         (out(128, 128), out(8 * NROW, 128), out(160, 640), out(800, 128), out(160, 640)),
         [vmem(200, 512), vmem(200, 640), vmem(1000, 128), vmem(200, 640)],
     )
-    ng, own, buf_s, buf_d, buf_sd = call(
+    ng, kern, buf_s = call(
         late_kernel,
         "late",
         (ha, stiff, spread, fold, wcol, kern_low, ng_low, mass, targ, val_up, prod_up, frc_up),
-        (out(8 * NROW, 128), out(256, 128), out(400, 128), out(328, 128), out(272, 128)),
-        [vmem(128, 128), vmem(200, 512), vmem(40, 640),
+        (out(8 * NROW, 128), out(128, 128), out(400, 128)),
+        [vmem(200, 512), vmem(40, 640),
          vmem(1000, 128), vmem(200, 640)],
     )
     got_s = send(buf_s, 1, 0, True, True)
+    own, buf_d, buf_sd = call(
+        pick_kernel,
+        "pick",
+        (kern_low, kern, ng_low, ng, mass, targ),
+        (out(256, 128), out(328, 128), out(272, 128)),
+    )
     got_d = send(buf_d, 0, 1, True, True)
     got_sd = send(buf_sd, 1, 1, False, False)
     field = out(4 * PLANE, 128)

time: 26.6 us -> 26.6 us (level)
    pallas_call x6 -> x7, Pallas kernels: 8.67 us -> 8.69 us  [call(): pl.pallas_call(kernel, out_shape=tuple(outs), in_specs=specs or [here] *...]
where the time goes in v6:
time: 26.6 us; the launch traced here: 26.3 us
  Pallas kernels  8.69 us (33%)
  starting transfers between devices  8.43 us (32%)
  waiting for transfers between devices  8.43 us (32%)
  between operations  0.75 us (3%)
    pallas_call x7, Pallas kernels, call(): pl.pallas_call(kernel, out_shape=tuple(outs), in_specs=specs or [here] *...  8.69 us
    ppermute x5, waiting for transfers between devices, send(): return lax.ppermute(x, ('surf', 'depth'), pairs)  8.43 us
    ppermute x5, starting transfers between devices, send(): return lax.ppermute(x, ('surf', 'depth'), pairs)  8.43 us
  transfers between devices with their start and end apart: 5, of which 3 were waited for; matrix products, arithmetic and copies ran while one was open for 0% of the time, Pallas kernels for 21%

profile of v6, /device:TPU:7, one launch (start us, length us, event | category | flops | bytes accessed | tf_op | source)
XLA Modules:
  0.0 26.3 jit_solution(3673431608898306954)
XLA Ops:
  0.6 0.9 %pack.1 = (f32[8,8,128]{2,1,0:T(8,128)S(1)}, f32[8,16,128]{2,1,0:T(8,128)S(1)}) custom-call(f32[4,8,16,128]{3,2,1,0:T(8,128)} %wave.1, f32[4,8,16,128]{3,2,1,0:T(8,128)} %adj.1), custom_call_target="tpu_custom_call" | custom-call | tf_op jit(solution)/shard_map/pack/pallas_call | solution.py:441
  1.5 0.7 %collective-permute-start = (f32[8,8,128]{2,0,1:T(8,128)S(1)}, f32[8,8,128]{2,0,1:T(8,128)S(1)}, u32[]{:S(2)}, u32[]{:S(2)}) collective-permute-start(f32[8,8,128]{2,0,1:T(8,128)S(1)} %copy.18), channel_id=1, source_target_pairs={{0,7},{1,0},{2,1},{3,2},{4,3},{5,4},{6,5},{7,6},{8,15},{9,8},{10,9... | collective-permute-start | bytes 98312 | tf_op jit(solution)/shard_map/ppermute | solution.py:435
  2.2 2.0 %prep.1 = (f32[1088,128]{1,0:T(8,128)S(1)}, f32[128,256]{1,0:T(8,128)S(1)}, f32[160,128]{1,0:T(8,128)S(1)}, f32[8,256]{1,0:T(8,128)S(1)}, bf16[512,512]{1,0:T(8,...) custom-call(f32[512,128]{1,0:T(8,128)} %bitcast.24, f32[512,128]{1,0:T(8,128)} %bitcast.25, ...), custom_call_target="tpu_custom_call" | custom-call | tf_op jit(solution)/shard_map/prep/pallas_call | solution.py:441
  4.2 1.9 %collective-permute-done = f32[8,8,128]{2,0,1:T(8,128)S(1)} collective-permute-done((f32[8,8,128]{2,0,1:T(8,128)S(1)}, f32[8,8,128]{2,0,1:T(8,128)S(1)}, u32[]{:S(2)}, u32[]{:S(2)}) %collective-permute-start) | collective-permute-done | bytes 32800 | tf_op jit(solution)/shard_map/ppermute | solution.py:435
  6.1 6.3 %collective-permute-start.1 = (f32[136,128]{1,0:T(8,128)S(1)}, f32[136,128]{1,0:T(8,128)S(1)}, u32[]{:S(2)}, u32[]{:S(2)}) collective-permute-start(f32[136,128]{1,0:T(8,128)S(1)} %pad_maximum_fusion), channel_id=1, source_target_pairs={{0,120},{1,121},{2,122},{3,123},{4,124},{5,125},{6,126},{7,127},{8... | collective-permute-start | bytes 208904 | tf_op jit(solution)/shard_map/ppermute | solution.py:435
  12.4 2.1 %early.1 = (f32[128,128]{1,0:T(8,128)S(1)}, f32[680,128]{1,0:T(8,128)S(1)}, f32[160,640]{1,0:T(8,128)S(1)}, f32[800,128]{1,0:T(8,128)S(1)}, f32[160,640]{1,0:T(8,128)S(1)}) custom-call(f32[1088,128]{1,0:T(8,128)S(1)} %get-tuple-element.48.fields, f32[64,128]{1,0:T(8,128)S(1)} %bitcast.22, f32[128,256]{1,0:T(8,128)S(1)} %get-tuple-element.50.stiff, ...), custom_call_target="tpu_custom_call" | custom-call | tf_op jit(solution)/shard_map/early/pallas_call | solution.py:441
  14.5 0.0 collective-permute-done.1.ha
  14.5 0.0 copy-start.3
  14.5 1.0 %late.1 = (f32[680,128]{1,0:T(8,128)S(1)}, f32[128,128]{1,0:T(8,128)S(1)}, f32[400,128]{1,0:T(8,128)S(1)}) custom-call(f32[136,128]{1,0:T(8,128)S(1)} %collective-permute-done.1.ha, f32[128,256]{1,0:T(8,128)S(1)} %get-tuple-element.50.stiff, bf16[512,512]{1,0:T(8,128)(2,1)S(1)} %get-tuple-element.51.spread, bf16[512,512]{1,0:T(8,128)(2,1)S(1)} %get-tuple-element.52.fold, ...), custom_call_target="tpu_custom_call" | custom-call | tf_op jit(solution)/shard_map/late/pallas_call | solution.py:441
  15.5 0.1 collective-permute-start.3
  15.6 0.0 copy-start
  15.6 0.0 copy-start.1
  15.6 0.0 copy-start.2
  15.6 0.1 pick.1
  15.7 0.7 %collective-permute-start.2 = (f32[328,128]{1,0:T(8,128)S(1)}, f32[328,128]{1,0:T(8,128)S(1)}, u32[]{:S(2)}, u32[]{:S(2)}) collective-permute-start(f32[328,128]{1,0:T(8,128)S(1)} %get-tuple-element.65), channel_id=1, source_target_pairs={{0,1},{1,2},{2,3},{3,4},{4,5},{5,6},{6,7},{7,0},{8,9},{9,10},{10,1... | collective-permute-start | bytes 503816 | tf_op jit(solution)/shard_map/ppermute | solution.py:435
  16.4 0.7 %collective-permute-start.4 = (f32[272,128]{1,0:T(8,128)S(1)}, f32[272,128]{1,0:T(8,128)S(1)}, u32[]{:S(2)}, u32[]{:S(2)}) collective-permute-start(f32[272,128]{1,0:T(8,128)S(1)} %get-tuple-element.69), channel_id=1, source_target_pairs={{0,9},{1,10},{2,11},{3,12},{4,13},{5,14},{6,15},{8,17},{9,18},{10,... | collective-permute-start | bytes 417800 | tf_op jit(solution)/shard_map/ppermute | solution.py:435
  17.1 1.6 %collective-permute-done.2.got_d = f32[328,128]{1,0:T(8,128)S(1)} collective-permute-done((f32[328,128]{1,0:T(8,128)S(1)}, f32[328,128]{1,0:T(8,128)S(1)}, u32[]{:S(2)}, u32[]{:S(2)}) %collective-permute-start.2) | collective-permute-done | bytes 167968 | tf_op jit(solution)/shard_map/ppermute | solution.py:435
  18.7 0.0 copy-done.3
  18.7 0.0 copy-done
  18.7 0.0 copy-done.1
  18.7 0.0 copy-done.2
  18.7 1.4 %near.1 = (f32[128,1024]{1,0:T(8,128)S(1)}, f32[9,16,128]{2,1,0:T(8,128)S(1)}, f32[512,128]{1,0:T(8,128)}, f32[512,128]{1,0:T(8,128)}) custom-call(f32[256,128]{1,0:T(8,128)S(1)} %get-tuple-element.64.own, f32[328,128]{1,0:T(8,128)S(1)} %collective-permute-done.2.got_d, f32[680,128]{1,0:T(8,128)S(1)} %get-tuple-element.56.ng_low, ...), custom_call_target="tpu_custom_call" | custom-call | tf_op jit(solution)/shard_map/near/pallas_call | solution.py:441
  20.1 0.0 collective-permute-done.4.got_sd
  20.1 4.9 %collective-permute-done.3.got_s = f32[400,128]{1,0:T(8,128)S(1)} collective-permute-done((f32[400,128]{1,0:T(8,128)S(1)}, f32[400,128]{1,0:T(8,128)S(1)}, u32[]{:S(2)}, u32[]{:S(2)}) %collective-permute-start.3) | collective-permute-done | bytes 204832 | tf_op jit(solution)/shard_map/ppermute | solution.py:435
  25.1 1.3 %final.1 = (f32[512,128]{1,0:T(8,128)}, f32[512,128]{1,0:T(8,128)}, f32[125,1024]{1,0:T(8,128)}) custom-call(f32[1088,128]{1,0:T(8,128)S(1)} %get-tuple-element.48.fields, f32[512,128]{1,0:T(8,128)S(1)} %bitcast.15, f32[512,128]{1,0:T(8,128)S(1)} %bitcast.17, f32[512,128]{1,0:T(8,128)S(1)} %bitcast.19, ...), custom_call_target="tpu_custom_call", output_to_operand_aliasing={{0}: (9, {}), {1}: (10, {})} | custom-call | tf_op jit(solution)/shard_map/final/pallas_call | solution.py:441
  (4 shorter events, 0.0 us)
Async XLA Ops:
  1.5 4.6 %collective-permute-start = (f32[8,8,128]{2,0,1:T(8,128)S(1)}, f32[8,8,128]{2,0,1:T(8,128)S(1)}, u32[]{:S(2)}, u32[]{:S(2)}) collective-permute-start(f32[8,8,128]{2,0,1:T(8,128)S(1)} %copy.18), channel_id=1, source_target_pairs={{0,7},{1,0},{2,1},{3,2},{4,3},{5,4},{6,5},{7,6},{8,15},{9,8},{10,9... | collective-permute-start | bytes 98312 | tf_op jit(solution)/shard_map/ppermute | solution.py:435
  6.1 8.4 %collective-permute-start.1 = (f32[136,128]{1,0:T(8,128)S(1)}, f32[136,128]{1,0:T(8,128)S(1)}, u32[]{:S(2)}, u32[]{:S(2)}) collective-permute-start(f32[136,128]{1,0:T(8,128)S(1)} %pad_maximum_fusion), channel_id=1, source_target_pairs={{0,120},{1,121},{2,122},{3,123},{4,124},{5,125},{6,126},{7,127},{8... | collective-permute-start | bytes 208904 | tf_op jit(solution)/shard_map/ppermute | solution.py:435
  14.5 4.3 %copy-start.3 = (f32[4,8,16,128]{3,2,1,0:T(8,128)S(1)}, f32[4,8,16,128]{3,2,1,0:T(8,128)}, u32[]{:S(2)}) copy-start(f32[4,8,16,128]{3,2,1,0:T(8,128)} %param.17) | copy-start | bytes 786436
  15.5 9.6 %collective-permute-start.3 = (f32[400,128]{1,0:T(8,128)S(1)}, f32[400,128]{1,0:T(8,128)S(1)}, u32[]{:S(2)}, u32[]{:S(2)}) collective-permute-start(f32[400,128]{1,0:T(8,128)S(1)} %get-tuple-element.68), channel_id=1, source_target_pairs={{0,8},{1,9},{2,10},{3,11},{4,12},{5,13},{6,14},{7,15},{8,16},{9,17... | collective-permute-start | bytes 614408 | tf_op jit(solution)/shard_map/ppermute | solution.py:435
  15.6 3.1 %copy-start = (f32[4,8,16,128]{3,2,1,0:T(8,128)S(1)}, f32[4,8,16,128]{3,2,1,0:T(8,128)}, u32[]{:S(2)}) copy-start(f32[4,8,16,128]{3,2,1,0:T(8,128)} %param.13) | copy-start | bytes 786436
  15.6 3.1 %copy-start.1 = (f32[4,8,16,128]{3,2,1,0:T(8,128)S(1)}, f32[4,8,16,128]{3,2,1,0:T(8,128)}, u32[]{:S(2)}) copy-start(f32[4,8,16,128]{3,2,1,0:T(8,128)} %param.15) | copy-start | bytes 786436
  15.6 3.1 %copy-start.2 = (f32[4,8,16,128]{3,2,1,0:T(8,128)S(1)}, f32[4,8,16,128]{3,2,1,0:T(8,128)}, u32[]{:S(2)}) copy-start(f32[4,8,16,128]{3,2,1,0:T(8,128)} %param.16) | copy-start | bytes 786436
  15.7 3.0 %collective-permute-start.2 = (f32[328,128]{1,0:T(8,128)S(1)}, f32[328,128]{1,0:T(8,128)S(1)}, u32[]{:S(2)}, u32[]{:S(2)}) collective-permute-start(f32[328,128]{1,0:T(8,128)S(1)} %get-tuple-element.65), channel_id=1, source_target_pairs={{0,1},{1,2},{2,3},{3,4},{4,5},{5,6},{6,7},{7,0},{8,9},{9,10},{10,1... | collective-permute-start | bytes 503816 | tf_op jit(solution)/shard_map/ppermute | solution.py:435
  16.4 3.7 %collective-permute-start.4 = (f32[272,128]{1,0:T(8,128)S(1)}, f32[272,128]{1,0:T(8,128)S(1)}, u32[]{:S(2)}, u32[]{:S(2)}) collective-permute-start(f32[272,128]{1,0:T(8,128)S(1)} %get-tuple-element.69), channel_id=1, source_target_pairs={{0,9},{1,10},{2,11},{3,12},{4,13},{5,14},{6,15},{8,17},{9,18},{10,... | collective-permute-start | bytes 417800 | tf_op jit(solution)/shard_map/ppermute | solution.py:435
